TPU v7x, 256 devices: a whole 4x4x8 slice. The times are simulated.
256 devices in a mesh: mp: 16 (over y, z_hi, core), replica: 16 (over x, z_lo).
Axes of the slice: x: 4, y: 4, z: 8 (z_hi: 2, z_lo: 4; z = z_hi * 4 + z_lo), core: 2. Of those that a mesh axis runs over, the one named last changes fastest.
Arguments:
- weight: float32 [2560, 5120], P('mp'), may hold values from -6 to 6
- first_moment: bfloat16 [16, 2560, 5120], P('replica', 'mp'), may hold values from -0.0011978149 to 0.0011978149
- second_moment: bfloat16 [16, 2560, 5120], P('replica', 'mp'), may hold values from 9.95351e-09 to 9.983778e-07
- outer_momentum: float32 [2560, 5120], P(('mp', 'replica')), may hold values from -0.3 to 0.3
- act_table: bfloat16 [2048, 5120], P(None, 'mp'), may hold values from -6 to 6
- token_ids: int32 [16, 2, 512], P('replica'), may hold values from 0 to 2047
- targets: bfloat16 [16, 2, 512, 2560], P('replica', None, None, 'mp'), may hold values from -6 to 6
Outputs:
- new_weight: float32 [2560, 5120], P('mp')
- momentum: float32 [2560, 5120], P(('mp', 'replica'))
All inputs are finite; a program needn't handle non-finite values. Where the computation divides by a largest or mean magnitude, that divisor is 1e-20 or more.
Results may differ from a plain program's by a relative error of at most 0.002.
Values may be sent and summed in bfloat16 or wider, within the bound.
No kernel may reach another device: no remote copies, remote signals or barrier semaphores. Data moves between devices by JAX's collectives and lax.ppermute only.
A program may use at most 64 MiB of HBM per device.

v0:
```python
import functools

import jax
import jax.numpy as jnp
from jax import lax
from jax.experimental import pallas as pl
from jax.experimental.pallas import tpu as pltpu
from jax.sharding import Mesh, PartitionSpec as P


STEPS = 2
BLOCK = 128
PRIOR_STEPS = 3

beta_first = 0.9
beta_second = 0.95
adam_epsilon = 1e-08
inner_rate = 0.1
weight_decay = 0.1
outer_mu = 0.9
outer_rate = 0.7
scale_epsilon = 1e-06

ROWS = 160
WIDTH = 5120
TOK = 512
CHUNK = 320
PAIR = 2 * CHUNK
SLOTS = 8
NEAR = 4
TILE = 32
COLS = 256
HALF = WIDTH // 2
PAYLOAD = HALF + BLOCK
QROWS = ROWS // 4
OWN = ROWS // 16

F32 = jnp.float32
BF16 = jnp.bfloat16
FACTOR = WIDTH ** (-0.5)
SCALE = FACTOR / TOK


HB = pl.BlockSpec(memory_space=pltpu.HBM)
VM = pl.BlockSpec(memory_space=pltpu.VMEM)
SM = pl.BlockSpec(memory_space=pltpu.SMEM)


def params(mib):
    return pltpu.CompilerParams(vmem_limit_bytes=mib << 20)


def gather_kernel(where_ref, ids_ref, table_ref, out_ref, total):
    step = 512
    total[...] = jnp.zeros_like(total)

    def body(block, carry):
        start = pl.multiple_of(block * step, step)
        row = lax.broadcasted_iota(jnp.int32, (step, TOK), 0) + start
        pick = jnp.where(row == ids_ref[...], 1.0, 0.0).astype(BF16)
        total[...] += jnp.dot(table_ref[:, pl.ds(start, step)], pick, preferred_element_type=F32)
        return carry

    lax.fori_loop(0, table_ref.shape[1] // step, body, 0)
    out_ref[...] = total[...].astype(BF16)


def gather(where, ids, table_t):
    return pl.pallas_call(
        gather_kernel,
        out_shape=jax.ShapeDtypeStruct((CHUNK, TOK), BF16),
        in_specs=[SM, VM, VM],
        out_specs=VM,
        scratch_shapes=[pltpu.VMEM((CHUNK, TOK), F32)],
        compiler_params=params(16),
        name="gather",
    )(where, ids, table_t)


def pack_kernel(*refs):
    out_ref = refs[-1]
    rows = refs[0].shape[0]
    for index, ref in enumerate(refs[:-1]):
        out_ref[index * rows : (index + 1) * rows, :] = ref[...]


def pack(*chunks):
    rows, width = chunks[0].shape
    return pl.pallas_call(
        pack_kernel,
        out_shape=jax.ShapeDtypeStruct((len(chunks) * rows, width), chunks[0].dtype),
        in_specs=[VM] * len(chunks),
        out_specs=VM,
        compiler_params=params(8),
        name="pack",
    )(*chunks)


def forward_kernel(half, counts, step, where_ref, extra_ref, w_ref, *refs):
    stacks = refs[: 2 * len(counts)]
    out_ref, x_ref, total = refs[2 * len(counts) : 2 * len(counts) + 3]
    core = where_ref[SLOTS]
    total[...] = jnp.zeros_like(total) if half == 0 else extra_ref[...]
    done = 0
    for group, count in enumerate(counts):

        def body(place, carry, group=group, done=done):
            slot = done + place
            rows = pl.ds(pl.multiple_of(place * CHUNK, CHUNK), CHUNK)
            base = slot * PAIR
            for index, at in enumerate((core, 1 - core)):
                to = pl.ds(pl.multiple_of(base + at * CHUNK, CHUNK), CHUNK)
                x_ref[to, :] = stacks[2 * group + index][rows, :]
            if w_ref.shape[1] == WIDTH:
                column = where_ref[half * NEAR + slot] * PAIR
            else:
                column = base
            weight = w_ref[:, pl.ds(pl.multiple_of(column, PAIR), PAIR)].astype(BF16)
            total[...] += jnp.dot(
                weight, x_ref[pl.ds(pl.multiple_of(base, PAIR), PAIR), :], preferred_element_type=F32
            )
            return carry

        lax.fori_loop(0, count, body, 0)
        done += count
    if half == 0:
        out_ref[...] = total[...]
    else:
        target_ref = refs[2 * len(counts) + 3]
        out_ref[...] = (total[...] * FACTOR - target_ref[step].astype(F32)).astype(BF16)


def forward_near_kernel(counts, step, where_ref, w_ref, *refs):
    forward_kernel(0, counts, step, where_ref, None, w_ref, *refs)


def forward_rest_kernel(counts, step, where_ref, total_ref, target_ref, w_ref, *refs):
    forward_kernel(1, counts, step, where_ref, total_ref, w_ref, *refs, target_ref)


def forward(half, step, where, extra, weight, xs):
    flat = [ref for pair in xs for ref in pair]
    counts = tuple(own.shape[0] // CHUNK for own, _ in xs)
    kernel = (forward_near_kernel, forward_rest_kernel)[half]
    return pl.pallas_call(
        functools.partial(kernel, counts, step),
        out_shape=(
            jax.ShapeDtypeStruct((ROWS, TOK), (F32, BF16)[half]),
            jax.ShapeDtypeStruct((HALF, TOK), BF16),
        ),
        in_specs=[SM] + [VM] * (len(extra) + 1 + len(flat)),
        out_specs=(VM, VM),
        scratch_shapes=[pltpu.VMEM((ROWS, TOK), F32)],
        compiler_params=params(24),
        cost_estimate=pl.CostEstimate(
            flops=ROWS * WIDTH * TOK, bytes_accessed=5 << 20, transcendentals=0
        ),
        name="forward",
    )(where, *extra, weight, *flat)


def corrections(step_count):
    return 1.0 / (1.0 - beta_first**step_count), 1.0 / (1.0 - beta_second**step_count)


def first_adam(product, one, two, weight):
    first, second = corrections(PRIOR_STEPS + 1)
    one = beta_first * one + ((1.0 - beta_first) * SCALE) * product
    two = beta_second * two + ((1.0 - beta_second) * SCALE * SCALE) * (product * product)
    update = (one * first) / (jnp.sqrt(two * second) + adam_epsilon)
    current = (1.0 - inner_rate * weight_decay) * weight - inner_rate * update
    first, second = corrections(PRIOR_STEPS + 2)
    kept = weight - (1.0 - inner_rate * weight_decay) * current
    return current, one * (beta_first * first), two * (beta_second * second), kept


def second_adam(product, one, two, kept):
    first, second = corrections(PRIOR_STEPS + 2)
    one = one + ((1.0 - beta_first) * first * SCALE) * product
    two = two + ((1.0 - beta_second) * second * SCALE * SCALE) * (product * product)
    return kept + inner_rate * (one / (jnp.sqrt(two) + adam_epsilon))


def backward(signal_ref, x_ref, grad, consume):
    steps = HALF // COLS

    def product(step, place):
        rows = pl.ds(pl.multiple_of(step * COLS, COLS), COLS)
        grad[place] = lax.dot_general(
            signal_ref[...], x_ref[rows, :], (((1,), (1,)), ((), ())), preferred_element_type=F32
        )

    product(0, 0)

    def body(step, carry):
        product(jnp.minimum(step + 1, steps - 1), (step + 1) % 2)
        for part in range(COLS // BLOCK):
            consume(step * (COLS // BLOCK) + part, part, step % 2)
        return carry

    lax.fori_loop(0, steps, body, 0)


def first_back_kernel(half, where_ref, signal_ref, x_ref, w_ref, one_ref, two_ref, *refs):
    cur_ref, *outs, grad = refs
    per = PAIR // BLOCK

    def consume(block, part, place):
        column = where_ref[half * NEAR + block // per] * PAIR + (block % per) * BLOCK
        source = pl.ds(pl.multiple_of(column, BLOCK), BLOCK)
        to = pl.ds(pl.multiple_of(block * BLOCK, BLOCK), BLOCK)
        for row in range(0, ROWS, TILE):
            rows = slice(row, row + TILE)
            current, *values = first_adam(
                grad[place, rows, part * BLOCK : (part + 1) * BLOCK],
                one_ref[rows, source].astype(F32),
                two_ref[rows, source].astype(F32),
                w_ref[rows, source],
            )
            cur_ref[rows, to] = current.astype(BF16)
            for out, value in zip(outs, values):
                out[rows, to] = value

    backward(signal_ref, x_ref, grad, consume)


def first_back(half, where, signal, x, weight, one, two):
    state = jax.ShapeDtypeStruct((ROWS, HALF), F32)
    return pl.pallas_call(
        functools.partial(first_back_kernel, half),
        out_shape=(jax.ShapeDtypeStruct((ROWS, HALF), BF16), state, state, state),
        in_specs=[SM] + [VM] * 5,
        out_specs=(VM,) * 4,
        scratch_shapes=[pltpu.VMEM((2, ROWS, COLS), F32)],
        compiler_params=params(24),
        cost_estimate=pl.CostEstimate(
            flops=ROWS * WIDTH * TOK, bytes_accessed=14 << 20, transcendentals=0
        ),
        name="first_back",
    )(where, signal, x, weight, one, two)


def second_back_kernel(where_ref, signal_ref, x_ref, one_ref, two_ref, kept_ref, *refs):
    outs = refs[:4]
    grad, scale_buf, code_buf = refs[4:]
    scale_buf[...] = jnp.zeros_like(scale_buf)
    lane = lax.broadcasted_iota(jnp.int32, (QROWS, BLOCK), 1)

    def consume(block, part, place):
        here = pl.ds(pl.multiple_of(block * BLOCK, BLOCK), BLOCK)
        for quarter in range(4):
            rows = slice(quarter * QROWS, (quarter + 1) * QROWS)
            delta = second_adam(
                grad[place, rows, part * BLOCK : (part + 1) * BLOCK],
                one_ref[rows, here],
                two_ref[rows, here],
                kept_ref[rows, here],
            )
            top = jnp.max(jnp.abs(delta), axis=1, keepdims=True) + scale_epsilon
            scale = jnp.broadcast_to(top.astype(BF16).astype(F32), (QROWS, BLOCK))
            code_buf[quarter, :, here] = (delta / scale).astype(BF16)
            scale_buf[quarter] = jnp.where(lane == block, scale, scale_buf[quarter])

    backward(signal_ref, x_ref, grad, consume)
    code_buf[:, :, HALF:] = scale_buf[...].astype(BF16)
    for by in range(4):
        outs[by][...] = code_buf[(where_ref[SLOTS + 1] + by) % 4]


def second_back(where, signal, x, state):
    return pl.pallas_call(
        second_back_kernel,
        out_shape=(jax.ShapeDtypeStruct((QROWS, PAYLOAD), BF16),) * 4,
        in_specs=[SM] + [VM] * 5,
        out_specs=(VM,) * 4,
        scratch_shapes=[
            pltpu.VMEM((2, ROWS, COLS), F32),
            pltpu.VMEM((4, QROWS, BLOCK), F32),
            pltpu.VMEM((4, QROWS, PAYLOAD), BF16),
        ],
        compiler_params=params(24),
        cost_estimate=pl.CostEstimate(
            flops=ROWS * WIDTH * TOK, bytes_accessed=14 << 20, transcendentals=0
        ),
        name="second_back",
    )(where, signal, x, *state)


def partial_kernel(where_ref, *refs):
    gots, outs = refs[:4], refs[4:8]
    part, piece = refs[8:]
    scales = [got[:, HALF:].astype(F32) for got in gots]
    for block in range(HALF // BLOCK):
        here = slice(block * BLOCK, (block + 1) * BLOCK)
        total = jnp.zeros((QROWS, BLOCK), F32)
        for got, scale in zip(gots, scales):
            total = total + got[:, here].astype(F32) * scale[:, block : block + 1]
        part[:, here] = total
    for line in range(4):
        for group in range(NEAR):
            piece[line, group * OWN : (group + 1) * OWN, :] = part[
                line * OWN : (line + 1) * OWN, group * PAIR : (group + 1) * PAIR
            ]
    for by in range(4):
        outs[by][...] = piece[(where_ref[SLOTS + 2] + by) % 4].astype(BF16)


def partial_sums(where, gots):
    return pl.pallas_call(
        partial_kernel,
        out_shape=(jax.ShapeDtypeStruct((QROWS, PAIR), BF16),) * 4,
        in_specs=[SM] + [VM] * 4,
        out_specs=(VM,) * 4,
        scratch_shapes=[
            pltpu.VMEM((QROWS, HALF), F32),
            pltpu.VMEM((4, QROWS, PAIR), F32),
        ],
        compiler_params=params(8),
        name="partial_sums",
    )(where, *gots)


def outer_kernel(half, where_ref, outer_ref, *refs):
    gots, refs = refs[:4], refs[4:]
    if half:
        before_ref, momentum_ref, code_ref, held, sent = refs
    else:
        sent, code_ref, held = refs

    def column(slot):
        return pl.ds(pl.multiple_of(where_ref[slot] * PAIR, PAIR), PAIR)

    for group in range(NEAR):
        held[group * OWN : (group + 1) * OWN, :] = outer_ref[:, column(half * NEAR + group)]
    lane = lax.broadcasted_iota(jnp.int32, (QROWS, BLOCK), 1)
    scales = jnp.zeros((QROWS, BLOCK), F32)
    for block in range(PAIR // BLOCK):
        here = slice(block * BLOCK, (block + 1) * BLOCK)
        total = gots[0][:, here].astype(F32)
        for got in gots[1:]:
            total = total + got[:, here].astype(F32)
        average = total * (1.0 / 16)
        momentum = outer_mu * held[:, here] + average
        sent[:, here] = momentum
        update = average + outer_mu * momentum
        top = jnp.max(jnp.abs(update), axis=1, keepdims=True) + scale_epsilon
        scale = jnp.broadcast_to(top.astype(BF16).astype(F32), (QROWS, BLOCK))
        code_ref[:, here] = (update / scale).astype(BF16)
        scales = jnp.where(lane == block, scale, scales)
    code_ref[:, PAIR:] = scales.astype(BF16)
    if half:
        for group in range(NEAR):
            rows = slice(group * OWN, (group + 1) * OWN)
            momentum_ref[:, column(group)] = before_ref[rows, :]
            momentum_ref[:, column(NEAR + group)] = sent[rows, :]


def outer_step(half, where, outer_momentum, gots, *before):
    momentum = ((QROWS, PAIR), (OWN, WIDTH))[half]
    return pl.pallas_call(
        functools.partial(outer_kernel, half),
        out_shape=(
            jax.ShapeDtypeStruct(momentum, F32),
            jax.ShapeDtypeStruct((QROWS, PAIR + BLOCK), BF16),
        ),
        in_specs=[SM] + [VM] * (5 + len(before)),
        out_specs=(VM, VM),
        scratch_shapes=[pltpu.VMEM((QROWS, PAIR), F32)] * (1 + half),
        compiler_params=params(8),
        name="outer_step",
    )(where, outer_momentum, *gots, *before)


def line_kernel(where_ref, *refs):
    pieces, out_ref, stack = refs[:4], refs[4], refs[5]
    for index, piece in enumerate(pieces):
        stack[index * QROWS : (index + 1) * QROWS, :] = piece[...].astype(F32)
    to = lax.broadcasted_iota(jnp.int32, (ROWS, ROWS), 0)
    source = lax.broadcasted_iota(jnp.int32, (ROWS, ROWS), 1)
    group, line, row = to // QROWS, (to % QROWS) // OWN, to % OWN
    wanted = ((where_ref[SLOTS + 2] - line + 4) % 4) * QROWS + group * OWN + row
    order = jnp.where(source == wanted, 1.0, 0.0).astype(BF16)
    rows = jnp.dot(order, stack[...].astype(BF16), preferred_element_type=F32)
    for group in range(NEAR):
        out_ref[group] = rows[group * QROWS : (group + 1) * QROWS, :].astype(BF16)


def line_rows(where, *pieces):
    return pl.pallas_call(
        line_kernel,
        out_shape=jax.ShapeDtypeStruct((NEAR, QROWS, PAIR + BLOCK), BF16),
        in_specs=[SM] + [VM] * 4,
        out_specs=VM,
        scratch_shapes=[pltpu.VMEM((ROWS, PAIR + BLOCK), F32)],
        compiler_params=params(8),
        name="line_rows",
    )(where, *pieces)


def final_kernel(where_ref, w_ref, *refs):
    pieces = refs[:8]
    out_ref, new_buf, out_sem = refs[8:]
    x = where_ref[SLOTS + 1]
    copies = []
    for by in (0, 1, 3, 2):
        rows = pl.ds(pl.multiple_of(((x - by + 4) % 4) * QROWS, 8), QROWS)

        def slots(group, carry, rows=rows, by=by):
            for half in range(2):
                piece = pieces[half * 4 + by]
                scales = piece[group, :, PAIR:].astype(F32)
                base = where_ref[half * NEAR + group] * PAIR
                for block in range(PAIR // BLOCK):
                    at = pl.ds(pl.multiple_of(base + block * BLOCK, BLOCK), BLOCK)
                    codes = piece[group, :, block * BLOCK : (block + 1) * BLOCK].astype(F32)
                    new_buf[rows, at] = w_ref[rows, at] - outer_rate * (codes * scales[:, block : block + 1])
            return carry

        lax.fori_loop(0, NEAR, slots, 0)
        copies.append(pltpu.make_async_copy(new_buf.at[rows], out_ref.at[rows], out_sem.at[by]))
        copies[-1].start()
    for copy in copies:
        copy.wait()


def final_step(where, weight, pieces):
    return pl.pallas_call(
        final_kernel,
        out_shape=jax.ShapeDtypeStruct((ROWS, WIDTH), F32),
        in_specs=[SM, VM] + [VM] * 8,
        out_specs=HB,
        scratch_shapes=[pltpu.VMEM((ROWS, WIDTH), F32), pltpu.SemaphoreType.DMA((4,))],
        compiler_params=params(16),
        name="final_step",
    )(where, weight, *pieces)


def shift(value, axis, by):
    size = lax.axis_size(axis)
    return lax.ppermute(value, axis, [(i, (i + by) % size) for i in range(size)])


def shifts(values, axis):
    return [shift(value, axis, by) for by, value in zip((1, 2, 3), values)]


def after(value, *others):
    return lax.optimization_barrier((value,) + others)[0]


def swap(own):
    return own, shift(own, "c", 1)


def window(weight, first_moment, second_moment, outer_momentum, act_table, token_ids, targets):
    y, zh, core = lax.axis_index("y"), lax.axis_index("zh"), lax.axis_index("c")
    x, zl = lax.axis_index("x"), lax.axis_index("zl")
    step_y = jnp.array([0, 0, -1, 1, 2, -1, 1, 2, 0, 0, 0], jnp.int32)
    step_z = jnp.array([0, 1, 0, 0, 0, 1, 1, 1, 0, 0, 0], jnp.int32)
    chip = ((y + step_y + 4) % 4) * 2 + (zh + step_z) % 2
    entry = jnp.arange(11)
    where = jnp.where(entry == 8, core, jnp.where(entry == 9, x, jnp.where(entry == 10, zl, chip)))
    where = where.astype(jnp.int32)

    table_t = act_table.T
    ids = token_ids[0]
    wanted = jnp.transpose(targets[0], (0, 2, 1))
    moments = (first_moment[0], second_moment[0])
    own1, own2 = [gather(where, ids[step : step + 1], table_t) for step in range(STEPS)]

    far1 = shift(own1, "zh", 1)
    left1, right1 = shift(own1, "y", 1), shift(own1, "y", -1)
    left2, right2 = shift(own2, "y", 1), shift(own2, "y", -1)
    opposite1, opposite2 = shift(left1, "y", 1), shift(right2, "y", -1)
    far2 = shift(own2, "zh", 1)
    far_left1, far_right1 = shift(far1, "y", 1), shift(far1, "y", -1)
    near1 = swap(pack(own1, far1, left1, right1))
    far_opposite1 = shift(far_right1, "y", -1)
    far_left2 = shift(far2, "y", 1)
    rest1 = swap(pack(opposite1, far_left1, far_right1, far_opposite1))
    total, near1 = forward(0, 0, where, (), weight, [near1])
    far_right2 = shift(after(far2, far_opposite1), "y", -1)
    near2 = swap(pack(own2, far2, left2, right2))
    signal, rest1 = forward(1, 0, where, (total, wanted), weight, [rest1])
    far_opposite2 = shift(far_left2, "y", 1)
    current0, *state0 = first_back(0, where, signal, near1, weight, *moments)
    rest2 = swap(pack(opposite2, far_left2, far_right2))
    current1, *state1 = first_back(1, where, signal, rest1, weight, *moments)
    last2 = swap(far_opposite2)
    total, near2 = forward(0, 1, where, (), current0, [near2])
    signal, rest2 = forward(1, 1, where, (total, wanted), current1, [rest2, last2])

    payloads = []
    for state, x_half in ((state0, near2), (state1, rest2)):
        sends = second_back(where, signal, x_half, state)
        payloads.append([sends[0]] + shifts(sends[1:], "x"))
    momentum, pieces = (), []
    for half in range(2):
        sends = partial_sums(where, payloads[half])
        sums = [sends[0]] + shifts(sends[1:], "zl")
        *momentum, codes = outer_step(half, where, outer_momentum, sums, *momentum)
        line = line_rows(where, codes, *shifts([codes] * 3, "zl"))
        left, right = shift(line, "x", 1), shift(line, "x", 3)
        opposite = shift((left, right)[half], "x", (1, 3)[half])
        pieces += [line, left, opposite, right]
    new_weight = final_step(where, weight, pieces)
    return (new_weight, momentum[0])


def solution(mesh):
    inner = Mesh(mesh.devices.reshape(4, 2, 2, 4, 4), ("y", "zh", "c", "x", "zl"))
    mp, replica = ("y", "zh", "c"), ("x", "zl")
    in_specs = (
        P(mp, None),
        P(replica, mp, None),
        P(replica, mp, None),
        P(mp + replica, None),
        P(None, mp),
        P(replica, None, None),
        P(replica, None, None, mp),
    )
    out_specs = (P(mp, None), P(mp + replica, None))
    return jax.shard_map(window, mesh=inner, in_specs=in_specs, out_specs=out_specs, check_vma=False)
```

profile of v0, /device:TPU:32, one launch (start us, length us, event | category | flops | bytes accessed | tf_op | source)
XLA Modules:
  0.0 186.0 jit_solution(9906671817553348790)
XLA Ops:
  5.4 6.4 %collective-permute-start = (bf16[320,512]{1,0:T(8,128)(2,1)S(1)}, bf16[320,512]{1,0:T(8,128)(2,1)S(1)}, u32[]{:S(2)}, u32[]{:S(2)}) collective-permute-start(bf16[320,512]{1,0:T(8,128)(2,1)S(1)} %gather.2.refs_0_), channel_id=1, source_target_pairs={{0,32},{32,0},{1,33},{33,1},{2,34},{34,2},{3,35},{35,3},{4,36},{36... | collective-permute-start | bytes 983048 | tf_op jit(solution)/shard_map/ppermute | solution.py:440
  13.4 13.2 %collective-permute-done.refs_1_ = bf16[320,512]{1,0:T(8,128)(2,1)S(1)} collective-permute-done((bf16[320,512]{1,0:T(8,128)(2,1)S(1)}, bf16[320,512]{1,0:T(8,128)(2,1)S(1)}, u32[]{:S(2)}, u32[]{:S(2)}) %collective-permute-start) | collective-permute-done | bytes 327712 | tf_op jit(solution)/shard_map/ppermute | solution.py:440
  26.6 3.0 %collective-permute-start.6 = (bf16[320,512]{1,0:T(8,128)(2,1)S(1)}, bf16[320,512]{1,0:T(8,128)(2,1)S(1)}, u32[]{:S(2)}, u32[]{:S(2)}) collective-permute-start(bf16[320,512]{1,0:T(8,128)(2,1)S(1)} %collective-permute-done.refs_1_), channel_id=1, source_target_pairs={{0,192},{64,0},{128,64},{192,128},{1,193},{65,1},{129,65},{193,129... | collective-permute-start | bytes 983048 | tf_op jit(solution)/shard_map/ppermute | solution.py:440
  32.3 5.6 %collective-permute-start.9 = (bf16[320,512]{1,0:T(8,128)(2,1)S(1)}, bf16[320,512]{1,0:T(8,128)(2,1)S(1)}, u32[]{:S(2)}, u32[]{:S(2)}) collective-permute-start(bf16[320,512]{1,0:T(8,128)(2,1)S(1)} %gather.3.refs_0_), channel_id=1, source_target_pairs={{0,32},{32,0},{1,33},{33,1},{2,34},{34,2},{3,35},{35,3},{4,36},{36... | collective-permute-start | bytes 983048 | tf_op jit(solution)/shard_map/ppermute | solution.py:440
  39.3 3.2 %collective-permute-start.7 = (bf16[320,512]{1,0:T(8,128)(2,1)S(1)}, bf16[320,512]{1,0:T(8,128)(2,1)S(1)}, u32[]{:S(2)}, u32[]{:S(2)}) collective-permute-start(bf16[320,512]{1,0:T(8,128)(2,1)S(1)} %collective-permute-done.6.refs_2_), channel_id=1, source_target_pairs={{0,192},{64,0},{128,64},{192,128},{1,193},{65,1},{129,65},{193,129... | collective-permute-start | bytes 983048 | tf_op jit(solution)/shard_map/ppermute | solution.py:440
  44.7 3.7 %collective-permute-start.11 = (bf16[320,512]{1,0:T(8,128)(2,1)S(1)}, bf16[320,512]{1,0:T(8,128)(2,1)S(1)}, u32[]{:S(2)}, u32[]{:S(2)}) collective-permute-start(bf16[320,512]{1,0:T(8,128)(2,1)S(1)} %gather.3.refs_0_), channel_id=1, source_target_pairs={{0,192},{64,0},{128,64},{192,128},{1,193},{65,1},{129,65},{193,129... | collective-permute-start | bytes 983048 | tf_op jit(solution)/shard_map/ppermute | solution.py:440
  56.3 6.6 %collective-permute-done.10.refs_2_ = bf16[320,512]{1,0:T(8,128)(2,1)S(1)} collective-permute-done((bf16[320,512]{1,0:T(8,128)(2,1)S(1)}, bf16[320,512]{1,0:T(8,128)(2,1)S(1)}, u32[]{:S(2)}, u32[]{:S(2)}) %collective-permute-start.10) | collective-permute-done | bytes 327712 | tf_op jit(solution)/shard_map/ppermute | solution.py:440
  63.1 5.3 %collective-permute-done.14.refs_1_ = bf16[320,512]{1,0:T(8,128)(2,1)S(1)} collective-permute-done((bf16[320,512]{1,0:T(8,128)(2,1)S(1)}, bf16[320,512]{1,0:T(8,128)(2,1)S(1)}, u32[]{:S(2)}, u32[]{:S(2)}) %collective-permute-start.14) | collective-permute-done | bytes 327712 | tf_op jit(solution)/shard_map/ppermute | solution.py:440
  68.5 5.2 %collective-permute-done.13.refs_0_ = bf16[320,512]{1,0:T(8,128)(2,1)S(1)} collective-permute-done((bf16[320,512]{1,0:T(8,128)(2,1)S(1)}, bf16[320,512]{1,0:T(8,128)(2,1)S(1)}, u32[]{:S(2)}, u32[]{:S(2)}) %collective-permute-start.13) | collective-permute-done | bytes 327712 | tf_op jit(solution)/shard_map/ppermute | solution.py:440
  73.7 6.5 %collective-permute-done.15.refs_2_ = bf16[320,512]{1,0:T(8,128)(2,1)S(1)} collective-permute-done((bf16[320,512]{1,0:T(8,128)(2,1)S(1)}, bf16[320,512]{1,0:T(8,128)(2,1)S(1)}, u32[]{:S(2)}, u32[]{:S(2)}) %collective-permute-start.15) | collective-permute-done | bytes 327712 | tf_op jit(solution)/shard_map/ppermute | solution.py:440
  80.5 11.2 %collective-permute-done.17.refs_2_ = bf16[320,512]{1,0:T(8,128)(2,1)S(1)} collective-permute-done((bf16[320,512]{1,0:T(8,128)(2,1)S(1)}, bf16[320,512]{1,0:T(8,128)(2,1)S(1)}, u32[]{:S(2)}, u32[]{:S(2)}) %collective-permute-start.17) | collective-permute-done | bytes 327712 | tf_op jit(solution)/shard_map/ppermute | solution.py:440
  95.8 4.9 %first_back.3 = (bf16[160,2560]{1,0:T(8,128)(2,1)S(1)}, f32[160,2560]{1,0:T(8,128)S(1)}, f32[160,2560]{1,0:T(8,128)S(1)}, f32[160,2560]{1,0:T(8,128)S(1)}) custom-call(s32[11]{0:T(128)S(1)} %compare_select_fusion.6.where_ref, bf16[160,512]{1,0:T(8,128)(2,1)S(1)} %get-tuple-element.40.signal_ref, bf16[2560,512]{1,0:T(8,128)(2,1)S(1)} %get-tuple-element.44.x_ref, ...), custom_call_target="tpu_custom_call" | custom-call | flops 419430400 | bytes 14680064 | tf_op jit(solution)/shard_map/first_back/pallas_call | solution.py:229
  100.7 4.9 %first_back.2 = (bf16[160,2560]{1,0:T(8,128)(2,1)S(1)}, f32[160,2560]{1,0:T(8,128)S(1)}, f32[160,2560]{1,0:T(8,128)S(1)}, f32[160,2560]{1,0:T(8,128)S(1)}) custom-call(s32[11]{0:T(128)S(1)} %compare_select_fusion.6.where_ref, bf16[160,512]{1,0:T(8,128)(2,1)S(1)} %get-tuple-element.40.signal_ref, bf16[2560,512]{1,0:T(8,128)(2,1)S(1)} %get-tuple-element.41.x_ref, ...), custom_call_target="tpu_custom_call" | custom-call | flops 419430400 | bytes 14680064 | tf_op jit(solution)/shard_map/first_back/pallas_call | solution.py:229
  109.5 5.2 %second_back.2 = (bf16[40,2688]{1,0:T(8,128)(2,1)S(1)}, bf16[40,2688]{1,0:T(8,128)(2,1)S(1)}, bf16[40,2688]{1,0:T(8,128)(2,1)S(1)}, bf16[40,2688]{1,0:T(8,128)(2,1)S(1)}) custom-call(s32[11]{0:T(128)S(1)} %compare_select_fusion.6.where_ref, bf16[160,512]{1,0:T(8,128)(2,1)S(1)} %get-tuple-element.47.signal_ref, ...), custom_call_target="tpu_custom_call" | custom-call | flops 419430400 | bytes 14680064 | tf_op jit(solution)/shard_map/second_back/pallas_call | solution.py:271
  116.3 2.7 %collective-permute-start.20 = (bf16[40,2688]{1,0:T(8,128)(2,1)S(1)}, bf16[40,2688]{1,0:T(8,128)(2,1)S(1)}, u32[]{:S(2)}, u32[]{:S(2)}) collective-permute-start(bf16[40,2688]{1,0:T(8,128)(2,1)S(1)} %get-tuple-element.54), channel_id=1, source_target_pairs={{0,8},{4,12},{8,0},{12,4},{1,9},{5,13},{9,1},{13,5},{2,10},{6,14},... | collective-permute-start | bytes 645128 | tf_op jit(solution)/shard_map/ppermute | solution.py:440
  120.4 5.2 %second_back.3 = (bf16[40,2688]{1,0:T(8,128)(2,1)S(1)}, bf16[40,2688]{1,0:T(8,128)(2,1)S(1)}, bf16[40,2688]{1,0:T(8,128)(2,1)S(1)}, bf16[40,2688]{1,0:T(8,128)(2,1)S(1)}) custom-call(s32[11]{0:T(128)S(1)} %compare_select_fusion.6.where_ref, bf16[160,512]{1,0:T(8,128)(2,1)S(1)} %get-tuple-element.47.signal_ref, ...), custom_call_target="tpu_custom_call" | custom-call | flops 419430400 | bytes 14680064 | tf_op jit(solution)/shard_map/second_back/pallas_call | solution.py:271
  132.8 5.9 %collective-permute-done.31.refs_1_ = bf16[40,2688]{1,0:T(8,128)(2,1)S(1)} collective-permute-done((bf16[40,2688]{1,0:T(8,128)(2,1)S(1)}, bf16[40,2688]{1,0:T(8,128)(2,1)S(1)}, u32[]{:S(2)}, u32[]{:S(2)}) %collective-permute-start.31) | collective-permute-done | bytes 215072 | tf_op jit(solution)/shard_map/ppermute | solution.py:440
  150.3 2.9 %collective-permute-start.38 = (bf16[40,768]{1,0:T(8,128)(2,1)S(1)}, bf16[40,768]{1,0:T(8,128)(2,1)S(1)}, u32[]{:S(2)}, u32[]{:S(2)}) collective-permute-start(bf16[40,768]{1,0:T(8,128)(2,1)S(1)} %get-tuple-element.74.refs_0_), channel_id=1, source_target_pairs={{0,2},{1,3},{2,0},{3,1},{4,6},{5,7},{6,4},{7,5},{8,10},{9,11},{10,... | collective-permute-start | bytes 184328 | tf_op jit(solution)/shard_map/ppermute | solution.py:440
  157.9 3.0 %collective-permute-done.39.refs_3_ = bf16[40,768]{1,0:T(8,128)(2,1)S(1)} collective-permute-done((bf16[40,768]{1,0:T(8,128)(2,1)S(1)}, bf16[40,768]{1,0:T(8,128)(2,1)S(1)}, u32[]{:S(2)}, u32[]{:S(2)}) %collective-permute-start.39) | collective-permute-done | bytes 61472 | tf_op jit(solution)/shard_map/ppermute | solution.py:440
  165.7 2.7 %collective-permute-start.30 = (bf16[4,40,768]{2,1,0:T(8,128)(2,1)S(1)}, bf16[4,40,768]{2,1,0:T(8,128)(2,1)S(1)}, u32[]{:S(2)}, u32[]{:S(2)}) collective-permute-start(bf16[4,40,768]{2,1,0:T(8,128)(2,1)S(1)} %line_rows.2.refs_0_), channel_id=1, source_target_pairs={{0,12},{4,0},{8,4},{12,8},{1,13},{5,1},{9,5},{13,9},{2,14},{6,2},{... | collective-permute-start | bytes 737288 | tf_op jit(solution)/shard_map/ppermute | solution.py:440
  170.2 3.5 %collective-permute-start.42 = (bf16[4,40,768]{2,1,0:T(8,128)(2,1)S(1)}, bf16[4,40,768]{2,1,0:T(8,128)(2,1)S(1)}, u32[]{:S(2)}, u32[]{:S(2)}) collective-permute-start(bf16[4,40,768]{2,1,0:T(8,128)(2,1)S(1)} %collective-permute-done.41.refs_7_), channel_id=1, source_target_pairs={{0,12},{4,0},{8,4},{12,8},{1,13},{5,1},{9,5},{13,9},{2,14},{6,2},{... | collective-permute-start | bytes 737288 | tf_op jit(solution)/shard_map/ppermute | solution.py:440
  175.1 3.8 %collective-permute-done.40.refs_5_ = bf16[4,40,768]{2,1,0:T(8,128)(2,1)S(1)} collective-permute-done((bf16[4,40,768]{2,1,0:T(8,128)(2,1)S(1)}, bf16[4,40,768]{2,1,0:T(8,128)(2,1)S(1)}, u32[]{:S(2)}, u32[]{:S(2)}) %collective-permute-start.40) | collective-permute-done | bytes 245792 | tf_op jit(solution)/shard_map/ppermute | solution.py:440
  178.9 3.6 %collective-permute-done.29.refs_2_ = bf16[4,40,768]{2,1,0:T(8,128)(2,1)S(1)} collective-permute-done((bf16[4,40,768]{2,1,0:T(8,128)(2,1)S(1)}, bf16[4,40,768]{2,1,0:T(8,128)(2,1)S(1)}, u32[]{:S(2)}, u32[]{:S(2)}) %collective-permute-start.29) | collective-permute-done | bytes 245792 | tf_op jit(solution)/shard_map/ppermute | solution.py:440
  182.5 3.3 %final_step.1 = f32[160,5120]{1,0:T(8,128)} custom-call(s32[11]{0:T(128)S(1)} %compare_select_fusion.6.where_ref, f32[160,5120]{1,0:T(8,128)S(1)} %copy-done, bf16[4,40,768]{2,1,0:T(8,128)(2,1)S(1)} %line_rows.2.refs_0_, bf16[4,40,768]{2,1,0:T(8,128)(2,1)S(1)} %collective-permute-done.28.refs_1_, bf16[4,40,768]{2,1,0:T(8,128)(2,1)S(1)} %collective-permute-done.29.refs_2_, ...), custom_call_target="tpu_custom_call" | custom-call | tf_op jit(solution)/shard_map/final_step/pallas_call | solution.py:427
  (99 shorter events, 63.4 us)
Async XLA Ops:
  5.4 21.2 %collective-permute-start = (bf16[320,512]{1,0:T(8,128)(2,1)S(1)}, bf16[320,512]{1,0:T(8,128)(2,1)S(1)}, u32[]{:S(2)}, u32[]{:S(2)}) collective-permute-start(bf16[320,512]{1,0:T(8,128)(2,1)S(1)} %gather.2.refs_0_), channel_id=1, source_target_pairs={{0,32},{32,0},{1,33},{33,1},{2,34},{34,2},{3,35},{35,3},{4,36},{36... | collective-permute-start | bytes 983048 | tf_op jit(solution)/shard_map/ppermute | solution.py:440
  11.8 27.5 %collective-permute-start.1 = (bf16[320,512]{1,0:T(8,128)(2,1)S(1)}, bf16[320,512]{1,0:T(8,128)(2,1)S(1)}, u32[]{:S(2)}, u32[]{:S(2)}) collective-permute-start(bf16[320,512]{1,0:T(8,128)(2,1)S(1)} %gather.2.refs_0_), channel_id=1, source_target_pairs={{0,64},{64,128},{128,192},{192,0},{1,65},{65,129},{129,193},{193,1... | collective-permute-start | bytes 983048 | tf_op jit(solution)/shard_map/ppermute | solution.py:440
  26.6 12.7 %collective-permute-start.6 = (bf16[320,512]{1,0:T(8,128)(2,1)S(1)}, bf16[320,512]{1,0:T(8,128)(2,1)S(1)}, u32[]{:S(2)}, u32[]{:S(2)}) collective-permute-start(bf16[320,512]{1,0:T(8,128)(2,1)S(1)} %collective-permute-done.refs_1_), channel_id=1, source_target_pairs={{0,192},{64,0},{128,64},{192,128},{1,193},{65,1},{129,65},{193,129... | collective-permute-start | bytes 983048 | tf_op jit(solution)/shard_map/ppermute | solution.py:440
  29.6 15.1 %collective-permute-start.2 = (bf16[320,512]{1,0:T(8,128)(2,1)S(1)}, bf16[320,512]{1,0:T(8,128)(2,1)S(1)}, u32[]{:S(2)}, u32[]{:S(2)}) collective-permute-start(bf16[320,512]{1,0:T(8,128)(2,1)S(1)} %gather.2.refs_0_), channel_id=1, source_target_pairs={{0,192},{64,0},{128,64},{192,128},{1,193},{65,1},{129,65},{193,129... | collective-permute-start | bytes 983048 | tf_op jit(solution)/shard_map/ppermute | solution.py:440
  32.3 18.7 %collective-permute-start.9 = (bf16[320,512]{1,0:T(8,128)(2,1)S(1)}, bf16[320,512]{1,0:T(8,128)(2,1)S(1)}, u32[]{:S(2)}, u32[]{:S(2)}) collective-permute-start(bf16[320,512]{1,0:T(8,128)(2,1)S(1)} %gather.3.refs_0_), channel_id=1, source_target_pairs={{0,32},{32,0},{1,33},{33,1},{2,34},{34,2},{3,35},{35,3},{4,36},{36... | collective-permute-start | bytes 983048 | tf_op jit(solution)/shard_map/ppermute | solution.py:440
  38.0 14.4 %collective-permute-start.5 = (bf16[320,512]{1,0:T(8,128)(2,1)S(1)}, bf16[320,512]{1,0:T(8,128)(2,1)S(1)}, u32[]{:S(2)}, u32[]{:S(2)}) collective-permute-start(bf16[320,512]{1,0:T(8,128)(2,1)S(1)} %collective-permute-done.refs_1_), channel_id=1, source_target_pairs={{0,64},{64,128},{128,192},{192,0},{1,65},{65,129},{129,193},{193,1... | collective-permute-start | bytes 983048 | tf_op jit(solution)/shard_map/ppermute | solution.py:440
  39.3 14.0 %collective-permute-start.4 = (bf16[320,512]{1,0:T(8,128)(2,1)S(1)}, bf16[320,512]{1,0:T(8,128)(2,1)S(1)}, u32[]{:S(2)}, u32[]{:S(2)}) collective-permute-start(bf16[320,512]{1,0:T(8,128)(2,1)S(1)} %collective-permute-done.1.refs_2_), channel_id=1, source_target_pairs={{0,64},{64,128},{128,192},{192,0},{1,65},{65,129},{129,193},{193,1... | collective-permute-start | bytes 983048 | tf_op jit(solution)/shard_map/ppermute | solution.py:440
  39.3 14.0 %collective-permute-start.7 = (bf16[320,512]{1,0:T(8,128)(2,1)S(1)}, bf16[320,512]{1,0:T(8,128)(2,1)S(1)}, u32[]{:S(2)}, u32[]{:S(2)}) collective-permute-start(bf16[320,512]{1,0:T(8,128)(2,1)S(1)} %collective-permute-done.6.refs_2_), channel_id=1, source_target_pairs={{0,192},{64,0},{128,64},{192,128},{1,193},{65,1},{129,65},{193,129... | collective-permute-start | bytes 983048 | tf_op jit(solution)/shard_map/ppermute | solution.py:440
  51.1 11.8 %collective-permute-start.10 = (bf16[320,512]{1,0:T(8,128)(2,1)S(1)}, bf16[320,512]{1,0:T(8,128)(2,1)S(1)}, u32[]{:S(2)}, u32[]{:S(2)}) collective-permute-start(bf16[320,512]{1,0:T(8,128)(2,1)S(1)} %gather.3.refs_0_), channel_id=1, source_target_pairs={{0,64},{64,128},{128,192},{192,0},{1,65},{65,129},{129,193},{193,1... | collective-permute-start | bytes 983048 | tf_op jit(solution)/shard_map/ppermute | solution.py:440
  52.4 16.1 %collective-permute-start.14 = (bf16[320,512]{1,0:T(8,128)(2,1)S(1)}, bf16[320,512]{1,0:T(8,128)(2,1)S(1)}, u32[]{:S(2)}, u32[]{:S(2)}) collective-permute-start(bf16[320,512]{1,0:T(8,128)(2,1)S(1)} %collective-permute-done.9.refs_1_), channel_id=1, source_target_pairs={{0,64},{64,128},{128,192},{192,0},{1,65},{65,129},{129,193},{193,1... | collective-permute-start | bytes 983048 | tf_op jit(solution)/shard_map/ppermute | solution.py:440
  53.3 38.4 %collective-permute-start.3 = (bf16[1280,512]{1,0:T(8,128)(2,1)S(1)}, bf16[1280,512]{1,0:T(8,128)(2,1)S(1)}, u32[]{:S(2)}, u32[]{:S(2)}) collective-permute-start(bf16[1280,512]{1,0:T(8,128)(2,1)S(1)} %pack.4.refs_0_), channel_id=1, source_target_pairs={{0,16},{16,0},{1,17},{17,1},{2,18},{18,2},{3,19},{19,3},{4,20},{20... | collective-permute-start | bytes 3932168 | tf_op jit(solution)/shard_map/ppermute | solution.py:440
  53.4 40.3 %collective-permute-start.8 = (bf16[1280,512]{1,0:T(8,128)(2,1)S(1)}, bf16[1280,512]{1,0:T(8,128)(2,1)S(1)}, u32[]{:S(2)}, u32[]{:S(2)}) collective-permute-start(bf16[1280,512]{1,0:T(8,128)(2,1)S(1)} %pack.5.refs_0_), channel_id=1, source_target_pairs={{0,16},{16,0},{1,17},{17,1},{2,18},{18,2},{3,19},{19,3},{4,20},{20... | collective-permute-start | bytes 3932168 | tf_op jit(solution)/shard_map/ppermute | solution.py:440
  63.0 42.6 %collective-permute-start.12 = (bf16[1280,512]{1,0:T(8,128)(2,1)S(1)}, bf16[1280,512]{1,0:T(8,128)(2,1)S(1)}, u32[]{:S(2)}, u32[]{:S(2)}) collective-permute-start(bf16[1280,512]{1,0:T(8,128)(2,1)S(1)} %pack.6.refs_0_), channel_id=1, source_target_pairs={{0,16},{16,0},{1,17},{17,1},{2,18},{18,2},{3,19},{19,3},{4,20},{20... | collective-permute-start | bytes 3932168 | tf_op jit(solution)/shard_map/ppermute | solution.py:440
  80.3 27.3 %collective-permute-start.16 = (bf16[960,512]{1,0:T(8,128)(2,1)S(1)}, bf16[960,512]{1,0:T(8,128)(2,1)S(1)}, u32[]{:S(2)}, u32[]{:S(2)}) collective-permute-start(bf16[960,512]{1,0:T(8,128)(2,1)S(1)} %pack.7.refs_0_), channel_id=1, source_target_pairs={{0,16},{16,0},{1,17},{17,1},{2,18},{18,2},{3,19},{19,3},{4,20},{20... | collective-permute-start | bytes 2949128 | tf_op jit(solution)/shard_map/ppermute | solution.py:440
  91.7 15.8 %collective-permute-start.18 = (bf16[320,512]{1,0:T(8,128)(2,1)S(1)}, bf16[320,512]{1,0:T(8,128)(2,1)S(1)}, u32[]{:S(2)}, u32[]{:S(2)}) collective-permute-start(bf16[320,512]{1,0:T(8,128)(2,1)S(1)} %collective-permute-done.17.refs_2_), channel_id=1, source_target_pairs={{0,16},{16,0},{1,17},{17,1},{2,18},{18,2},{3,19},{19,3},{4,20},{20... | collective-permute-start | bytes 983048 | tf_op jit(solution)/shard_map/ppermute | solution.py:440
  114.7 12.5 %collective-permute-start.19 = (bf16[40,2688]{1,0:T(8,128)(2,1)S(1)}, bf16[40,2688]{1,0:T(8,128)(2,1)S(1)}, u32[]{:S(2)}, u32[]{:S(2)}) collective-permute-start(bf16[40,2688]{1,0:T(8,128)(2,1)S(1)} %get-tuple-element.53), channel_id=1, source_target_pairs={{0,4},{4,8},{8,12},{12,0},{1,5},{5,9},{9,13},{13,1},{2,6},{6,10},{... | collective-permute-start | bytes 645128 | tf_op jit(solution)/shard_map/ppermute | solution.py:440
  116.3 13.5 %collective-permute-start.20 = (bf16[40,2688]{1,0:T(8,128)(2,1)S(1)}, bf16[40,2688]{1,0:T(8,128)(2,1)S(1)}, u32[]{:S(2)}, u32[]{:S(2)}) collective-permute-start(bf16[40,2688]{1,0:T(8,128)(2,1)S(1)} %get-tuple-element.54), channel_id=1, source_target_pairs={{0,8},{4,12},{8,0},{12,4},{1,9},{5,13},{9,1},{13,5},{2,10},{6,14},... | collective-permute-start | bytes 645128 | tf_op jit(solution)/shard_map/ppermute | solution.py:440
  125.6 13.1 %collective-permute-start.31 = (bf16[40,2688]{1,0:T(8,128)(2,1)S(1)}, bf16[40,2688]{1,0:T(8,128)(2,1)S(1)}, u32[]{:S(2)}, u32[]{:S(2)}) collective-permute-start(bf16[40,2688]{1,0:T(8,128)(2,1)S(1)} %get-tuple-element.66), channel_id=1, source_target_pairs={{0,4},{4,8},{8,12},{12,0},{1,5},{5,9},{9,13},{13,1},{2,6},{6,10},{... | collective-permute-start | bytes 645128 | tf_op jit(solution)/shard_map/ppermute | solution.py:440
  126.3 12.4 %collective-permute-start.32 = (bf16[40,2688]{1,0:T(8,128)(2,1)S(1)}, bf16[40,2688]{1,0:T(8,128)(2,1)S(1)}, u32[]{:S(2)}, u32[]{:S(2)}) collective-permute-start(bf16[40,2688]{1,0:T(8,128)(2,1)S(1)} %get-tuple-element.67), channel_id=1, source_target_pairs={{0,8},{4,12},{8,0},{12,4},{1,9},{5,13},{9,1},{13,5},{2,10},{6,14},... | collective-permute-start | bytes 645128 | tf_op jit(solution)/shard_map/ppermute | solution.py:440
  127.2 11.8 %collective-permute-start.33 = (bf16[40,2688]{1,0:T(8,128)(2,1)S(1)}, bf16[40,2688]{1,0:T(8,128)(2,1)S(1)}, u32[]{:S(2)}, u32[]{:S(2)}) collective-permute-start(bf16[40,2688]{1,0:T(8,128)(2,1)S(1)} %get-tuple-element.68), channel_id=1, source_target_pairs={{0,12},{4,0},{8,4},{12,8},{1,13},{5,1},{9,5},{13,9},{2,14},{6,2},{... | collective-permute-start | bytes 645128 | tf_op jit(solution)/shard_map/ppermute | solution.py:440
  130.7 13.6 %collective-permute-start.22 = (bf16[40,640]{1,0:T(8,128)(2,1)S(1)}, bf16[40,640]{1,0:T(8,128)(2,1)S(1)}, u32[]{:S(2)}, u32[]{:S(2)}) collective-permute-start(bf16[40,640]{1,0:T(8,128)(2,1)S(1)} %get-tuple-element.57), channel_id=1, source_target_pairs={{0,1},{1,2},{2,3},{3,0},{4,5},{5,6},{6,7},{7,4},{8,9},{9,10},{10,1... | collective-permute-start | bytes 153608 | tf_op jit(solution)/shard_map/ppermute | solution.py:440
  132.7 12.7 %collective-permute-start.23 = (bf16[40,640]{1,0:T(8,128)(2,1)S(1)}, bf16[40,640]{1,0:T(8,128)(2,1)S(1)}, u32[]{:S(2)}, u32[]{:S(2)}) collective-permute-start(bf16[40,640]{1,0:T(8,128)(2,1)S(1)} %get-tuple-element.58), channel_id=1, source_target_pairs={{0,2},{1,3},{2,0},{3,1},{4,6},{5,7},{6,4},{7,5},{8,10},{9,11},{10,... | collective-permute-start | bytes 153608 | tf_op jit(solution)/shard_map/ppermute | solution.py:440
  165.1 13.9 %collective-permute-start.40 = (bf16[4,40,768]{2,1,0:T(8,128)(2,1)S(1)}, bf16[4,40,768]{2,1,0:T(8,128)(2,1)S(1)}, u32[]{:S(2)}, u32[]{:S(2)}) collective-permute-start(bf16[4,40,768]{2,1,0:T(8,128)(2,1)S(1)} %line_rows.3.refs_4_), channel_id=1, source_target_pairs={{0,4},{4,8},{8,12},{12,0},{1,5},{5,9},{9,13},{13,1},{2,6},{6,10},{... | collective-permute-start | bytes 737288 | tf_op jit(solution)/shard_map/ppermute | solution.py:440
  165.7 13.2 %collective-permute-start.30 = (bf16[4,40,768]{2,1,0:T(8,128)(2,1)S(1)}, bf16[4,40,768]{2,1,0:T(8,128)(2,1)S(1)}, u32[]{:S(2)}, u32[]{:S(2)}) collective-permute-start(bf16[4,40,768]{2,1,0:T(8,128)(2,1)S(1)} %line_rows.2.refs_0_), channel_id=1, source_target_pairs={{0,12},{4,0},{8,4},{12,8},{1,13},{5,1},{9,5},{13,9},{2,14},{6,2},{... | collective-permute-start | bytes 737288 | tf_op jit(solution)/shard_map/ppermute | solution.py:440
  (26 other events, 264.6 us)
where the time goes:
time: 186 us
  waiting for transfers between devices  79.1 us (43%)
  starting transfers between devices  61.6 us (33%)
  Pallas kernels  41.3 us (22%)
  local copies, waits for them, and re-layouts  2.11 us (1%)
    ppermute x43, waiting for transfers between devices, shift(): lax.ppermute(value, axis, [(i, (i + by) % size) for i in range(size)])  79.1 us
    ppermute x43, starting transfers between devices, shift(): lax.ppermute(value, axis, [(i, (i + by) % size) for i in range(size)])  61.6 us
    pallas_call x2, Pallas kernels, second_back(): pl.pallas_call(second_back_kernel, out_shape=(jax.ShapeDtypeStruct((QROWS...  10.3 us
    pallas_call x2, Pallas kernels, first_back(): pl.pallas_call(functools.partial(first_back_kernel, half), out_shape=(jax...  9.76 us
    pallas_call x4, Pallas kernels, forward(): pl.pallas_call(functools.partial(kernel, counts, step), out_shape=(jax.Sh...  7.9 us
    pallas_call x2, Pallas kernels, gather(): pl.pallas_call(gather_kernel, out_shape=jax.ShapeDtypeStruct((CHUNK, TOK)...  3.95 us
  transfers between devices with their start and end apart: 43, of which 21 were waited for; matrix products, arithmetic and copies ran while one was open for 0% of the time, Pallas kernels for 15%

commit v1 on v0

--- a/solution.py
+++ b/solution.py
@@ -8,7 +8,6 @@
 from jax.sharding import Mesh, PartitionSpec as P
 
 
-STEPS = 2
 BLOCK = 128
 PRIOR_STEPS = 3
 
@@ -50,31 +49,32 @@
     return pltpu.CompilerParams(vmem_limit_bytes=mib << 20)
 
 
-def gather_kernel(where_ref, ids_ref, table_ref, out_ref, total):
-    step = 512
+def gather_kernel(step, unroll, ids_ref, table_ref, *refs):
+    out_ref, total = refs[-2:]
+    width = 512
     total[...] = jnp.zeros_like(total)
 
     def body(block, carry):
-        start = pl.multiple_of(block * step, step)
-        row = lax.broadcasted_iota(jnp.int32, (step, TOK), 0) + start
-        pick = jnp.where(row == ids_ref[...], 1.0, 0.0).astype(BF16)
-        total[...] += jnp.dot(table_ref[:, pl.ds(start, step)], pick, preferred_element_type=F32)
+        start = pl.multiple_of(block * width, width)
+        row = lax.broadcasted_iota(jnp.int32, (width, TOK), 0) + start
+        pick = jnp.where(row == ids_ref[step : step + 1, :], 1.0, 0.0).astype(BF16)
+        total[...] += jnp.dot(table_ref[:, pl.ds(start, width)], pick, preferred_element_type=F32)
         return carry
 
-    lax.fori_loop(0, table_ref.shape[1] // step, body, 0)
+    lax.fori_loop(0, table_ref.shape[1] // width, body, 0, unroll=unroll)
     out_ref[...] = total[...].astype(BF16)
 
 
-def gather(where, ids, table_t):
-    return pl.pallas_call(
-        gather_kernel,
+def gather(step, unroll, ids, table_t, *early):
+    return pl.pallas_call(
+        functools.partial(gather_kernel, step, unroll),
         out_shape=jax.ShapeDtypeStruct((CHUNK, TOK), BF16),
-        in_specs=[SM, VM, VM],
+        in_specs=[VM, VM] + [SM] * len(early),
         out_specs=VM,
         scratch_shapes=[pltpu.VMEM((CHUNK, TOK), F32)],
         compiler_params=params(16),
         name="gather",
-    )(where, ids, table_t)
+    )(ids, table_t, *early)
 
 
 def pack_kernel(*refs):
@@ -163,11 +163,15 @@
     return 1.0 / (1.0 - beta_first**step_count), 1.0 / (1.0 - beta_second**step_count)
 
 
+def root(value):
+    return value * lax.rsqrt(value)
+
+
 def first_adam(product, one, two, weight):
     first, second = corrections(PRIOR_STEPS + 1)
     one = beta_first * one + ((1.0 - beta_first) * SCALE) * product
     two = beta_second * two + ((1.0 - beta_second) * SCALE * SCALE) * (product * product)
-    update = (one * first) / (jnp.sqrt(two * second) + adam_epsilon)
+    update = (one * first) / (root(two * second) + adam_epsilon)
     current = (1.0 - inner_rate * weight_decay) * weight - inner_rate * update
     first, second = corrections(PRIOR_STEPS + 2)
     kept = weight - (1.0 - inner_rate * weight_decay) * current
@@ -178,7 +182,7 @@
     first, second = corrections(PRIOR_STEPS + 2)
     one = one + ((1.0 - beta_first) * first * SCALE) * product
     two = two + ((1.0 - beta_second) * second * SCALE * SCALE) * (product * product)
-    return kept + inner_rate * (one / (jnp.sqrt(two) + adam_epsilon))
+    return kept + inner_rate * (one / (root(two) + adam_epsilon))
 
 
 def backward(signal_ref, x_ref, grad, consume):
@@ -466,7 +470,8 @@
     ids = token_ids[0]
     wanted = jnp.transpose(targets[0], (0, 2, 1))
     moments = (first_moment[0], second_moment[0])
-    own1, own2 = [gather(where, ids[step : step + 1], table_t) for step in range(STEPS)]
+    own1 = gather(0, True, ids, table_t)
+    own2 = gather(1, False, ids, table_t, where)
 
     far1 = shift(own1, "zh", 1)
     left1, right1 = shift(own1, "y", 1), shift(own1, "y", -1)

time: 186 us -> 183 us (0.984)
  starting transfers between devices: 61.6 us -> 58.2 us
  waiting for transfers between devices: 79.1 us -> 81.8 us
  Pallas kernels: 41.3 us -> 39.4 us
    ppermute x43, starting transfers between devices: 61.6 us -> 58.2 us  [shift(): lax.ppermute(value, axis, [(i, (i + by) % size) for i in range(size)])]
    ppermute x43, waiting for transfers between devices: 79.1 us -> 81.8 us  [shift(): lax.ppermute(value, axis, [(i, (i + by) % size) for i in range(size)])]
  transfers between devices with their start and end apart: 43 -> 43, of which waited for: 21 -> 19; matrix products, arithmetic and copies ran while one was open for 0% -> 0% of each run, Pallas kernels for 15% -> 15%
where the time goes in v1:
time: 183 us
  waiting for transfers between devices  81.8 us (45%)
  starting transfers between devices  58.2 us (32%)
  Pallas kernels  39.4 us (22%)
  local copies, waits for them, and re-layouts  2.06 us (1%)
    ppermute x43, waiting for transfers between devices, shift(): lax.ppermute(value, axis, [(i, (i + by) % size) for i in range(size)])  81.8 us
    ppermute x43, starting transfers between devices, shift(): lax.ppermute(value, axis, [(i, (i + by) % size) for i in range(size)])  58.2 us
    pallas_call x2, Pallas kernels, second_back(): pl.pallas_call(second_back_kernel, out_shape=(jax.ShapeDtypeStruct((QROWS...  10.2 us
    pallas_call x2, Pallas kernels, first_back(): pl.pallas_call(functools.partial(first_back_kernel, half), out_shape=(jax...  9.17 us
    pallas_call x4, Pallas kernels, forward(): pl.pallas_call(functools.partial(kernel, counts, step), out_shape=(jax.Sh...  7.9 us
  transfers between devices with their start and end apart: 43, of which 19 were waited for; matrix products, arithmetic and copies ran while one was open for 0% of the time, Pallas kernels for 15%

profile of v1, /device:TPU:32, one launch (start us, length us, event | category | flops | bytes accessed | tf_op | source)
XLA Modules:
  0.0 182.7 jit_solution(4968924479477477244)
XLA Ops:
  3.5 6.4 %collective-permute-start = (bf16[320,512]{1,0:T(8,128)(2,1)S(1)}, bf16[320,512]{1,0:T(8,128)(2,1)S(1)}, u32[]{:S(2)}, u32[]{:S(2)}) collective-permute-start(bf16[320,512]{1,0:T(8,128)(2,1)S(1)} %gather.2.refs_0_), channel_id=1, source_target_pairs={{0,32},{32,0},{1,33},{33,1},{2,34},{34,2},{3,35},{35,3},{4,36},{36... | collective-permute-start | bytes 983048 | tf_op jit(solution)/shard_map/ppermute | solution.py:444
  13.1 11.6 %collective-permute-done.refs_1_ = bf16[320,512]{1,0:T(8,128)(2,1)S(1)} collective-permute-done((bf16[320,512]{1,0:T(8,128)(2,1)S(1)}, bf16[320,512]{1,0:T(8,128)(2,1)S(1)}, u32[]{:S(2)}, u32[]{:S(2)}) %collective-permute-start) | collective-permute-done | bytes 327712 | tf_op jit(solution)/shard_map/ppermute | solution.py:444
  24.7 3.0 %collective-permute-start.6 = (bf16[320,512]{1,0:T(8,128)(2,1)S(1)}, bf16[320,512]{1,0:T(8,128)(2,1)S(1)}, u32[]{:S(2)}, u32[]{:S(2)}) collective-permute-start(bf16[320,512]{1,0:T(8,128)(2,1)S(1)} %collective-permute-done.refs_1_), channel_id=1, source_target_pairs={{0,192},{64,0},{128,64},{192,128},{1,193},{65,1},{129,65},{193,129... | collective-permute-start | bytes 983048 | tf_op jit(solution)/shard_map/ppermute | solution.py:444
  29.8 5.6 %collective-permute-start.9 = (bf16[320,512]{1,0:T(8,128)(2,1)S(1)}, bf16[320,512]{1,0:T(8,128)(2,1)S(1)}, u32[]{:S(2)}, u32[]{:S(2)}) collective-permute-start(bf16[320,512]{1,0:T(8,128)(2,1)S(1)} %gather.3.refs_0_), channel_id=1, source_target_pairs={{0,32},{32,0},{1,33},{33,1},{2,34},{34,2},{3,35},{35,3},{4,36},{36... | collective-permute-start | bytes 983048 | tf_op jit(solution)/shard_map/ppermute | solution.py:444
  36.0 2.7 %collective-permute-start.7 = (bf16[320,512]{1,0:T(8,128)(2,1)S(1)}, bf16[320,512]{1,0:T(8,128)(2,1)S(1)}, u32[]{:S(2)}, u32[]{:S(2)}) collective-permute-start(bf16[320,512]{1,0:T(8,128)(2,1)S(1)} %collective-permute-done.6.refs_2_), channel_id=1, source_target_pairs={{0,192},{64,0},{128,64},{192,128},{1,193},{65,1},{129,65},{193,129... | collective-permute-start | bytes 983048 | tf_op jit(solution)/shard_map/ppermute | solution.py:444
  40.7 8.1 %collective-permute-done.9.refs_1_ = bf16[320,512]{1,0:T(8,128)(2,1)S(1)} collective-permute-done((bf16[320,512]{1,0:T(8,128)(2,1)S(1)}, bf16[320,512]{1,0:T(8,128)(2,1)S(1)}, u32[]{:S(2)}, u32[]{:S(2)}) %collective-permute-start.9) | collective-permute-done | bytes 327712 | tf_op jit(solution)/shard_map/ppermute | solution.py:444
  51.7 8.9 %collective-permute-done.10.refs_2_ = bf16[320,512]{1,0:T(8,128)(2,1)S(1)} collective-permute-done((bf16[320,512]{1,0:T(8,128)(2,1)S(1)}, bf16[320,512]{1,0:T(8,128)(2,1)S(1)}, u32[]{:S(2)}, u32[]{:S(2)}) %collective-permute-start.10) | collective-permute-done | bytes 327712 | tf_op jit(solution)/shard_map/ppermute | solution.py:444
  60.9 5.3 %collective-permute-done.14.refs_1_ = bf16[320,512]{1,0:T(8,128)(2,1)S(1)} collective-permute-done((bf16[320,512]{1,0:T(8,128)(2,1)S(1)}, bf16[320,512]{1,0:T(8,128)(2,1)S(1)}, u32[]{:S(2)}, u32[]{:S(2)}) %collective-permute-start.14) | collective-permute-done | bytes 327712 | tf_op jit(solution)/shard_map/ppermute | solution.py:444
  66.2 5.2 %collective-permute-done.13.refs_0_ = bf16[320,512]{1,0:T(8,128)(2,1)S(1)} collective-permute-done((bf16[320,512]{1,0:T(8,128)(2,1)S(1)}, bf16[320,512]{1,0:T(8,128)(2,1)S(1)}, u32[]{:S(2)}, u32[]{:S(2)}) %collective-permute-start.13) | collective-permute-done | bytes 327712 | tf_op jit(solution)/shard_map/ppermute | solution.py:444
  71.4 6.5 %collective-permute-done.15.refs_2_ = bf16[320,512]{1,0:T(8,128)(2,1)S(1)} collective-permute-done((bf16[320,512]{1,0:T(8,128)(2,1)S(1)}, bf16[320,512]{1,0:T(8,128)(2,1)S(1)}, u32[]{:S(2)}, u32[]{:S(2)}) %collective-permute-start.15) | collective-permute-done | bytes 327712 | tf_op jit(solution)/shard_map/ppermute | solution.py:444
  78.2 11.2 %collective-permute-done.17.refs_2_ = bf16[320,512]{1,0:T(8,128)(2,1)S(1)} collective-permute-done((bf16[320,512]{1,0:T(8,128)(2,1)S(1)}, bf16[320,512]{1,0:T(8,128)(2,1)S(1)}, u32[]{:S(2)}, u32[]{:S(2)}) %collective-permute-start.17) | collective-permute-done | bytes 327712 | tf_op jit(solution)/shard_map/ppermute | solution.py:444
  93.5 4.6 %first_back.3 = (bf16[160,2560]{1,0:T(8,128)(2,1)S(1)}, f32[160,2560]{1,0:T(8,128)S(1)}, f32[160,2560]{1,0:T(8,128)S(1)}, f32[160,2560]{1,0:T(8,128)S(1)}) custom-call(s32[11]{0:T(128)S(1)} %compare_select_fusion.6.where_ref.refs_0_, bf16[160,512]{1,0:T(8,128)(2,1)S(1)} %get-tuple-element.40.signal_ref, bf16[2560,512]{1,0:T(8,128)(2,1)S(1)} %get-tuple-element.44.x_ref, ...), custom_call_target="tpu_custom_call" | custom-call | flops 419430400 | bytes 14680064 | tf_op jit(solution)/shard_map/first_back/pallas_call | solution.py:233
  98.1 4.6 %first_back.2 = (bf16[160,2560]{1,0:T(8,128)(2,1)S(1)}, f32[160,2560]{1,0:T(8,128)S(1)}, f32[160,2560]{1,0:T(8,128)S(1)}, f32[160,2560]{1,0:T(8,128)S(1)}) custom-call(s32[11]{0:T(128)S(1)} %compare_select_fusion.6.where_ref.refs_0_, bf16[160,512]{1,0:T(8,128)(2,1)S(1)} %get-tuple-element.40.signal_ref, bf16[2560,512]{1,0:T(8,128)(2,1)S(1)} %get-tuple-element.41.x_ref, ...), custom_call_target="tpu_custom_call" | custom-call | flops 419430400 | bytes 14680064 | tf_op jit(solution)/shard_map/first_back/pallas_call | solution.py:233
  106.6 5.1 %second_back.2 = (bf16[40,2688]{1,0:T(8,128)(2,1)S(1)}, bf16[40,2688]{1,0:T(8,128)(2,1)S(1)}, bf16[40,2688]{1,0:T(8,128)(2,1)S(1)}, bf16[40,2688]{1,0:T(8,128)(2,1)S(1)}) custom-call(s32[11]{0:T(128)S(1)} %compare_select_fusion.6.where_ref.refs_0_, bf16[160,512]{1,0:T(8,128)(2,1)S(1)} %get-tuple-element.47.signal_ref, ...), custom_call_target="tpu_custom_call" | custom-call | flops 419430400 | bytes 14680064 | tf_op jit(solution)/shard_map/second_back/pallas_call | solution.py:275
  113.3 2.8 %collective-permute-start.20 = (bf16[40,2688]{1,0:T(8,128)(2,1)S(1)}, bf16[40,2688]{1,0:T(8,128)(2,1)S(1)}, u32[]{:S(2)}, u32[]{:S(2)}) collective-permute-start(bf16[40,2688]{1,0:T(8,128)(2,1)S(1)} %get-tuple-element.54), channel_id=1, source_target_pairs={{0,8},{4,12},{8,0},{12,4},{1,9},{5,13},{9,1},{13,5},{2,10},{6,14},... | collective-permute-start | bytes 645128 | tf_op jit(solution)/shard_map/ppermute | solution.py:444
  117.5 5.1 %second_back.3 = (bf16[40,2688]{1,0:T(8,128)(2,1)S(1)}, bf16[40,2688]{1,0:T(8,128)(2,1)S(1)}, bf16[40,2688]{1,0:T(8,128)(2,1)S(1)}, bf16[40,2688]{1,0:T(8,128)(2,1)S(1)}) custom-call(s32[11]{0:T(128)S(1)} %compare_select_fusion.6.where_ref.refs_0_, bf16[160,512]{1,0:T(8,128)(2,1)S(1)} %get-tuple-element.47.signal_ref, ...), custom_call_target="tpu_custom_call" | custom-call | flops 419430400 | bytes 14680064 | tf_op jit(solution)/shard_map/second_back/pallas_call | solution.py:275
  129.5 6.2 %collective-permute-done.31.refs_1_ = bf16[40,2688]{1,0:T(8,128)(2,1)S(1)} collective-permute-done((bf16[40,2688]{1,0:T(8,128)(2,1)S(1)}, bf16[40,2688]{1,0:T(8,128)(2,1)S(1)}, u32[]{:S(2)}, u32[]{:S(2)}) %collective-permute-start.31) | collective-permute-done | bytes 215072 | tf_op jit(solution)/shard_map/ppermute | solution.py:444
  147.0 2.9 %collective-permute-start.38 = (bf16[40,768]{1,0:T(8,128)(2,1)S(1)}, bf16[40,768]{1,0:T(8,128)(2,1)S(1)}, u32[]{:S(2)}, u32[]{:S(2)}) collective-permute-start(bf16[40,768]{1,0:T(8,128)(2,1)S(1)} %get-tuple-element.74.refs_0_), channel_id=1, source_target_pairs={{0,2},{1,3},{2,0},{3,1},{4,6},{5,7},{6,4},{7,5},{8,10},{9,11},{10,... | collective-permute-start | bytes 184328 | tf_op jit(solution)/shard_map/ppermute | solution.py:444
  154.6 3.0 %collective-permute-done.39.refs_3_ = bf16[40,768]{1,0:T(8,128)(2,1)S(1)} collective-permute-done((bf16[40,768]{1,0:T(8,128)(2,1)S(1)}, bf16[40,768]{1,0:T(8,128)(2,1)S(1)}, u32[]{:S(2)}, u32[]{:S(2)}) %collective-permute-start.39) | collective-permute-done | bytes 61472 | tf_op jit(solution)/shard_map/ppermute | solution.py:444
  162.4 2.7 %collective-permute-start.30 = (bf16[4,40,768]{2,1,0:T(8,128)(2,1)S(1)}, bf16[4,40,768]{2,1,0:T(8,128)(2,1)S(1)}, u32[]{:S(2)}, u32[]{:S(2)}) collective-permute-start(bf16[4,40,768]{2,1,0:T(8,128)(2,1)S(1)} %line_rows.2.refs_0_), channel_id=1, source_target_pairs={{0,12},{4,0},{8,4},{12,8},{1,13},{5,1},{9,5},{13,9},{2,14},{6,2},{... | collective-permute-start | bytes 737288 | tf_op jit(solution)/shard_map/ppermute | solution.py:444
  166.9 3.4 %collective-permute-start.42 = (bf16[4,40,768]{2,1,0:T(8,128)(2,1)S(1)}, bf16[4,40,768]{2,1,0:T(8,128)(2,1)S(1)}, u32[]{:S(2)}, u32[]{:S(2)}) collective-permute-start(bf16[4,40,768]{2,1,0:T(8,128)(2,1)S(1)} %collective-permute-done.41.refs_7_), channel_id=1, source_target_pairs={{0,12},{4,0},{8,4},{12,8},{1,13},{5,1},{9,5},{13,9},{2,14},{6,2},{... | collective-permute-start | bytes 737288 | tf_op jit(solution)/shard_map/ppermute | solution.py:444
  171.8 3.9 %collective-permute-done.40.refs_5_ = bf16[4,40,768]{2,1,0:T(8,128)(2,1)S(1)} collective-permute-done((bf16[4,40,768]{2,1,0:T(8,128)(2,1)S(1)}, bf16[4,40,768]{2,1,0:T(8,128)(2,1)S(1)}, u32[]{:S(2)}, u32[]{:S(2)}) %collective-permute-start.40) | collective-permute-done | bytes 245792 | tf_op jit(solution)/shard_map/ppermute | solution.py:444
  175.7 3.5 %collective-permute-done.29.refs_2_ = bf16[4,40,768]{2,1,0:T(8,128)(2,1)S(1)} collective-permute-done((bf16[4,40,768]{2,1,0:T(8,128)(2,1)S(1)}, bf16[4,40,768]{2,1,0:T(8,128)(2,1)S(1)}, u32[]{:S(2)}, u32[]{:S(2)}) %collective-permute-start.29) | collective-permute-done | bytes 245792 | tf_op jit(solution)/shard_map/ppermute | solution.py:444
  179.2 3.3 %final_step.1 = f32[160,5120]{1,0:T(8,128)} custom-call(s32[11]{0:T(128)S(1)} %compare_select_fusion.6.where_ref.refs_0_, f32[160,5120]{1,0:T(8,128)S(1)} %copy-done, bf16[4,40,768]{2,1,0:T(8,128)(2,1)S(1)} %line_rows.2.refs_0_, bf16[4,40,768]{2,1,0:T(8,128)(2,1)S(1)} %collective-permute-done.28.refs_1_, ...), custom_call_target="tpu_custom_call" | custom-call | tf_op jit(solution)/shard_map/final_step/pallas_call | solution.py:431
  (106 shorter events, 55.9 us)
Async XLA Ops:
  3.5 21.2 %collective-permute-start = (bf16[320,512]{1,0:T(8,128)(2,1)S(1)}, bf16[320,512]{1,0:T(8,128)(2,1)S(1)}, u32[]{:S(2)}, u32[]{:S(2)}) collective-permute-start(bf16[320,512]{1,0:T(8,128)(2,1)S(1)} %gather.2.refs_0_), channel_id=1, source_target_pairs={{0,32},{32,0},{1,33},{33,1},{2,34},{34,2},{3,35},{35,3},{4,36},{36... | collective-permute-start | bytes 983048 | tf_op jit(solution)/shard_map/ppermute | solution.py:444
  9.9 25.5 %collective-permute-start.1 = (bf16[320,512]{1,0:T(8,128)(2,1)S(1)}, bf16[320,512]{1,0:T(8,128)(2,1)S(1)}, u32[]{:S(2)}, u32[]{:S(2)}) collective-permute-start(bf16[320,512]{1,0:T(8,128)(2,1)S(1)} %gather.2.refs_0_), channel_id=1, source_target_pairs={{0,64},{64,128},{128,192},{192,0},{1,65},{65,129},{129,193},{193,1... | collective-permute-start | bytes 983048 | tf_op jit(solution)/shard_map/ppermute | solution.py:444
  11.5 27.3 %collective-permute-start.2 = (bf16[320,512]{1,0:T(8,128)(2,1)S(1)}, bf16[320,512]{1,0:T(8,128)(2,1)S(1)}, u32[]{:S(2)}, u32[]{:S(2)}) collective-permute-start(bf16[320,512]{1,0:T(8,128)(2,1)S(1)} %gather.2.refs_0_), channel_id=1, source_target_pairs={{0,192},{64,0},{128,64},{192,128},{1,193},{65,1},{129,65},{193,129... | collective-permute-start | bytes 983048 | tf_op jit(solution)/shard_map/ppermute | solution.py:444
  29.8 19.0 %collective-permute-start.9 = (bf16[320,512]{1,0:T(8,128)(2,1)S(1)}, bf16[320,512]{1,0:T(8,128)(2,1)S(1)}, u32[]{:S(2)}, u32[]{:S(2)}) collective-permute-start(bf16[320,512]{1,0:T(8,128)(2,1)S(1)} %gather.3.refs_0_), channel_id=1, source_target_pairs={{0,32},{32,0},{1,33},{33,1},{2,34},{34,2},{3,35},{35,3},{4,36},{36... | collective-permute-start | bytes 983048 | tf_op jit(solution)/shard_map/ppermute | solution.py:444
  35.4 13.4 %collective-permute-start.5 = (bf16[320,512]{1,0:T(8,128)(2,1)S(1)}, bf16[320,512]{1,0:T(8,128)(2,1)S(1)}, u32[]{:S(2)}, u32[]{:S(2)}) collective-permute-start(bf16[320,512]{1,0:T(8,128)(2,1)S(1)} %collective-permute-done.refs_1_), channel_id=1, source_target_pairs={{0,64},{64,128},{128,192},{192,0},{1,65},{65,129},{129,193},{193,1... | collective-permute-start | bytes 983048 | tf_op jit(solution)/shard_map/ppermute | solution.py:444
  35.4 15.6 %collective-permute-start.4 = (bf16[320,512]{1,0:T(8,128)(2,1)S(1)}, bf16[320,512]{1,0:T(8,128)(2,1)S(1)}, u32[]{:S(2)}, u32[]{:S(2)}) collective-permute-start(bf16[320,512]{1,0:T(8,128)(2,1)S(1)} %collective-permute-done.1.refs_2_), channel_id=1, source_target_pairs={{0,64},{64,128},{128,192},{192,0},{1,65},{65,129},{129,193},{193,1... | collective-permute-start | bytes 983048 | tf_op jit(solution)/shard_map/ppermute | solution.py:444
  36.0 15.0 %collective-permute-start.7 = (bf16[320,512]{1,0:T(8,128)(2,1)S(1)}, bf16[320,512]{1,0:T(8,128)(2,1)S(1)}, u32[]{:S(2)}, u32[]{:S(2)}) collective-permute-start(bf16[320,512]{1,0:T(8,128)(2,1)S(1)} %collective-permute-done.6.refs_2_), channel_id=1, source_target_pairs={{0,192},{64,0},{128,64},{192,128},{1,193},{65,1},{129,65},{193,129... | collective-permute-start | bytes 983048 | tf_op jit(solution)/shard_map/ppermute | solution.py:444
  38.7 13.0 %collective-permute-start.11 = (bf16[320,512]{1,0:T(8,128)(2,1)S(1)}, bf16[320,512]{1,0:T(8,128)(2,1)S(1)}, u32[]{:S(2)}, u32[]{:S(2)}) collective-permute-start(bf16[320,512]{1,0:T(8,128)(2,1)S(1)} %gather.3.refs_0_), channel_id=1, source_target_pairs={{0,192},{64,0},{128,64},{192,128},{1,193},{65,1},{129,65},{193,129... | collective-permute-start | bytes 983048 | tf_op jit(solution)/shard_map/ppermute | solution.py:444
  48.8 11.8 %collective-permute-start.10 = (bf16[320,512]{1,0:T(8,128)(2,1)S(1)}, bf16[320,512]{1,0:T(8,128)(2,1)S(1)}, u32[]{:S(2)}, u32[]{:S(2)}) collective-permute-start(bf16[320,512]{1,0:T(8,128)(2,1)S(1)} %gather.3.refs_0_), channel_id=1, source_target_pairs={{0,64},{64,128},{128,192},{192,0},{1,65},{65,129},{129,193},{193,1... | collective-permute-start | bytes 983048 | tf_op jit(solution)/shard_map/ppermute | solution.py:444
  48.8 17.4 %collective-permute-start.14 = (bf16[320,512]{1,0:T(8,128)(2,1)S(1)}, bf16[320,512]{1,0:T(8,128)(2,1)S(1)}, u32[]{:S(2)}, u32[]{:S(2)}) collective-permute-start(bf16[320,512]{1,0:T(8,128)(2,1)S(1)} %collective-permute-done.9.refs_1_), channel_id=1, source_target_pairs={{0,64},{64,128},{128,192},{192,0},{1,65},{65,129},{129,193},{193,1... | collective-permute-start | bytes 983048 | tf_op jit(solution)/shard_map/ppermute | solution.py:444
  51.0 38.4 %collective-permute-start.3 = (bf16[1280,512]{1,0:T(8,128)(2,1)S(1)}, bf16[1280,512]{1,0:T(8,128)(2,1)S(1)}, u32[]{:S(2)}, u32[]{:S(2)}) collective-permute-start(bf16[1280,512]{1,0:T(8,128)(2,1)S(1)} %pack.4.refs_0_), channel_id=1, source_target_pairs={{0,16},{16,0},{1,17},{17,1},{2,18},{18,2},{3,19},{19,3},{4,20},{20... | collective-permute-start | bytes 3932168 | tf_op jit(solution)/shard_map/ppermute | solution.py:444
  51.1 40.3 %collective-permute-start.8 = (bf16[1280,512]{1,0:T(8,128)(2,1)S(1)}, bf16[1280,512]{1,0:T(8,128)(2,1)S(1)}, u32[]{:S(2)}, u32[]{:S(2)}) collective-permute-start(bf16[1280,512]{1,0:T(8,128)(2,1)S(1)} %pack.5.refs_0_), channel_id=1, source_target_pairs={{0,16},{16,0},{1,17},{17,1},{2,18},{18,2},{3,19},{19,3},{4,20},{20... | collective-permute-start | bytes 3932168 | tf_op jit(solution)/shard_map/ppermute | solution.py:444
  60.7 42.0 %collective-permute-start.12 = (bf16[1280,512]{1,0:T(8,128)(2,1)S(1)}, bf16[1280,512]{1,0:T(8,128)(2,1)S(1)}, u32[]{:S(2)}, u32[]{:S(2)}) collective-permute-start(bf16[1280,512]{1,0:T(8,128)(2,1)S(1)} %pack.6.refs_0_), channel_id=1, source_target_pairs={{0,16},{16,0},{1,17},{17,1},{2,18},{18,2},{3,19},{19,3},{4,20},{20... | collective-permute-start | bytes 3932168 | tf_op jit(solution)/shard_map/ppermute | solution.py:444
  78.0 26.7 %collective-permute-start.16 = (bf16[960,512]{1,0:T(8,128)(2,1)S(1)}, bf16[960,512]{1,0:T(8,128)(2,1)S(1)}, u32[]{:S(2)}, u32[]{:S(2)}) collective-permute-start(bf16[960,512]{1,0:T(8,128)(2,1)S(1)} %pack.7.refs_0_), channel_id=1, source_target_pairs={{0,16},{16,0},{1,17},{17,1},{2,18},{18,2},{3,19},{19,3},{4,20},{20... | collective-permute-start | bytes 2949128 | tf_op jit(solution)/shard_map/ppermute | solution.py:444
  89.4 15.3 %collective-permute-start.18 = (bf16[320,512]{1,0:T(8,128)(2,1)S(1)}, bf16[320,512]{1,0:T(8,128)(2,1)S(1)}, u32[]{:S(2)}, u32[]{:S(2)}) collective-permute-start(bf16[320,512]{1,0:T(8,128)(2,1)S(1)} %collective-permute-done.17.refs_2_), channel_id=1, source_target_pairs={{0,16},{16,0},{1,17},{17,1},{2,18},{18,2},{3,19},{19,3},{4,20},{20... | collective-permute-start | bytes 983048 | tf_op jit(solution)/shard_map/ppermute | solution.py:444
  111.7 12.4 %collective-permute-start.19 = (bf16[40,2688]{1,0:T(8,128)(2,1)S(1)}, bf16[40,2688]{1,0:T(8,128)(2,1)S(1)}, u32[]{:S(2)}, u32[]{:S(2)}) collective-permute-start(bf16[40,2688]{1,0:T(8,128)(2,1)S(1)} %get-tuple-element.53), channel_id=1, source_target_pairs={{0,4},{4,8},{8,12},{12,0},{1,5},{5,9},{9,13},{13,1},{2,6},{6,10},{... | collective-permute-start | bytes 645128 | tf_op jit(solution)/shard_map/ppermute | solution.py:444
  113.3 13.5 %collective-permute-start.20 = (bf16[40,2688]{1,0:T(8,128)(2,1)S(1)}, bf16[40,2688]{1,0:T(8,128)(2,1)S(1)}, u32[]{:S(2)}, u32[]{:S(2)}) collective-permute-start(bf16[40,2688]{1,0:T(8,128)(2,1)S(1)} %get-tuple-element.54), channel_id=1, source_target_pairs={{0,8},{4,12},{8,0},{12,4},{1,9},{5,13},{9,1},{13,5},{2,10},{6,14},... | collective-permute-start | bytes 645128 | tf_op jit(solution)/shard_map/ppermute | solution.py:444
  122.6 13.1 %collective-permute-start.31 = (bf16[40,2688]{1,0:T(8,128)(2,1)S(1)}, bf16[40,2688]{1,0:T(8,128)(2,1)S(1)}, u32[]{:S(2)}, u32[]{:S(2)}) collective-permute-start(bf16[40,2688]{1,0:T(8,128)(2,1)S(1)} %get-tuple-element.66), channel_id=1, source_target_pairs={{0,4},{4,8},{8,12},{12,0},{1,5},{5,9},{9,13},{13,1},{2,6},{6,10},{... | collective-permute-start | bytes 645128 | tf_op jit(solution)/shard_map/ppermute | solution.py:444
  123.3 12.4 %collective-permute-start.32 = (bf16[40,2688]{1,0:T(8,128)(2,1)S(1)}, bf16[40,2688]{1,0:T(8,128)(2,1)S(1)}, u32[]{:S(2)}, u32[]{:S(2)}) collective-permute-start(bf16[40,2688]{1,0:T(8,128)(2,1)S(1)} %get-tuple-element.67), channel_id=1, source_target_pairs={{0,8},{4,12},{8,0},{12,4},{1,9},{5,13},{9,1},{13,5},{2,10},{6,14},... | collective-permute-start | bytes 645128 | tf_op jit(solution)/shard_map/ppermute | solution.py:444
  124.1 11.9 %collective-permute-start.33 = (bf16[40,2688]{1,0:T(8,128)(2,1)S(1)}, bf16[40,2688]{1,0:T(8,128)(2,1)S(1)}, u32[]{:S(2)}, u32[]{:S(2)}) collective-permute-start(bf16[40,2688]{1,0:T(8,128)(2,1)S(1)} %get-tuple-element.68), channel_id=1, source_target_pairs={{0,12},{4,0},{8,4},{12,8},{1,13},{5,1},{9,5},{13,9},{2,14},{6,2},{... | collective-permute-start | bytes 645128 | tf_op jit(solution)/shard_map/ppermute | solution.py:444
  127.8 13.2 %collective-permute-start.22 = (bf16[40,640]{1,0:T(8,128)(2,1)S(1)}, bf16[40,640]{1,0:T(8,128)(2,1)S(1)}, u32[]{:S(2)}, u32[]{:S(2)}) collective-permute-start(bf16[40,640]{1,0:T(8,128)(2,1)S(1)} %get-tuple-element.57), channel_id=1, source_target_pairs={{0,1},{1,2},{2,3},{3,0},{4,5},{5,6},{6,7},{7,4},{8,9},{9,10},{10,1... | collective-permute-start | bytes 153608 | tf_op jit(solution)/shard_map/ppermute | solution.py:444
  129.5 12.6 %collective-permute-start.23 = (bf16[40,640]{1,0:T(8,128)(2,1)S(1)}, bf16[40,640]{1,0:T(8,128)(2,1)S(1)}, u32[]{:S(2)}, u32[]{:S(2)}) collective-permute-start(bf16[40,640]{1,0:T(8,128)(2,1)S(1)} %get-tuple-element.58), channel_id=1, source_target_pairs={{0,2},{1,3},{2,0},{3,1},{4,6},{5,7},{6,4},{7,5},{8,10},{9,11},{10,... | collective-permute-start | bytes 153608 | tf_op jit(solution)/shard_map/ppermute | solution.py:444
  161.8 13.9 %collective-permute-start.40 = (bf16[4,40,768]{2,1,0:T(8,128)(2,1)S(1)}, bf16[4,40,768]{2,1,0:T(8,128)(2,1)S(1)}, u32[]{:S(2)}, u32[]{:S(2)}) collective-permute-start(bf16[4,40,768]{2,1,0:T(8,128)(2,1)S(1)} %line_rows.3.refs_4_), channel_id=1, source_target_pairs={{0,4},{4,8},{8,12},{12,0},{1,5},{5,9},{9,13},{13,1},{2,6},{6,10},{... | collective-permute-start | bytes 737288 | tf_op jit(solution)/shard_map/ppermute | solution.py:444
  162.4 13.3 %collective-permute-start.30 = (bf16[4,40,768]{2,1,0:T(8,128)(2,1)S(1)}, bf16[4,40,768]{2,1,0:T(8,128)(2,1)S(1)}, u32[]{:S(2)}, u32[]{:S(2)}) collective-permute-start(bf16[4,40,768]{2,1,0:T(8,128)(2,1)S(1)} %line_rows.2.refs_0_), channel_id=1, source_target_pairs={{0,12},{4,0},{8,4},{12,8},{1,13},{5,1},{9,5},{13,9},{2,14},{6,2},{... | collective-permute-start | bytes 737288 | tf_op jit(solution)/shard_map/ppermute | solution.py:444
  (30 other events, 341.6 us)

commit v2 on v1

--- a/solution.py
+++ b/solution.py
@@ -101,28 +101,36 @@
     out_ref, x_ref, total = refs[2 * len(counts) : 2 * len(counts) + 3]
     core = where_ref[SLOTS]
     total[...] = jnp.zeros_like(total) if half == 0 else extra_ref[...]
-    done = 0
-    for group, count in enumerate(counts):
-
-        def body(place, carry, group=group, done=done):
-            slot = done + place
-            rows = pl.ds(pl.multiple_of(place * CHUNK, CHUNK), CHUNK)
-            base = slot * PAIR
-            for index, at in enumerate((core, 1 - core)):
-                to = pl.ds(pl.multiple_of(base + at * CHUNK, CHUNK), CHUNK)
-                x_ref[to, :] = stacks[2 * group + index][rows, :]
-            if w_ref.shape[1] == WIDTH:
-                column = where_ref[half * NEAR + slot] * PAIR
-            else:
-                column = base
-            weight = w_ref[:, pl.ds(pl.multiple_of(column, PAIR), PAIR)].astype(BF16)
-            total[...] += jnp.dot(
-                weight, x_ref[pl.ds(pl.multiple_of(base, PAIR), PAIR), :], preferred_element_type=F32
-            )
-            return carry
-
-        lax.fori_loop(0, count, body, 0)
+
+    def ordered(slot, place, group):
+        rows = pl.ds(pl.multiple_of(place * CHUNK, CHUNK), CHUNK)
+        for index, at in enumerate((core, 1 - core)):
+            to = pl.ds(pl.multiple_of(slot * PAIR + at * CHUNK, CHUNK), CHUNK)
+            x_ref[to, :] = stacks[2 * group + index][rows, :]
+
+    done = counts[0]
+    for group, count in enumerate(counts[1:]):
+        for place in range(count):
+            ordered(done + place, place, group + 1)
         done += count
+
+    def body(slot, carry):
+        if len(counts) == 1:
+            ordered(slot, slot, 0)
+        else:
+            pl.when(slot < counts[0])(lambda: ordered(slot, slot, 0))
+        base = slot * PAIR
+        if w_ref.shape[1] == WIDTH:
+            column = where_ref[half * NEAR + slot] * PAIR
+        else:
+            column = base
+        weight = w_ref[:, pl.ds(pl.multiple_of(column, PAIR), PAIR)].astype(BF16)
+        total[...] += jnp.dot(
+            weight, x_ref[pl.ds(pl.multiple_of(base, PAIR), PAIR), :], preferred_element_type=F32
+        )
+        return carry
+
+    lax.fori_loop(0, NEAR, body, 0)
     if half == 0:
         out_ref[...] = total[...]
     else:
@@ -324,21 +332,23 @@
     )(where, *gots)
 
 
+def column(where_ref, slot):
+    return pl.ds(pl.multiple_of(where_ref[slot] * PAIR, PAIR), PAIR)
+
+
 def outer_kernel(half, where_ref, outer_ref, *refs):
     gots, refs = refs[:4], refs[4:]
     if half:
-        before_ref, momentum_ref, code_ref, held, sent = refs
+        scales_ref, sent, code_ref, held = refs
+        scales = scales_ref[...]
     else:
-        sent, code_ref, held = refs
-
-    def column(slot):
-        return pl.ds(pl.multiple_of(where_ref[slot] * PAIR, PAIR), PAIR)
-
+        sent, code_ref, scales_ref, held = refs
+        scales = jnp.zeros((QROWS, BLOCK), F32)
     for group in range(NEAR):
-        held[group * OWN : (group + 1) * OWN, :] = outer_ref[:, column(half * NEAR + group)]
+        held[group * OWN : (group + 1) * OWN, :] = outer_ref[:, column(where_ref, half * NEAR + group)]
     lane = lax.broadcasted_iota(jnp.int32, (QROWS, BLOCK), 1)
-    scales = jnp.zeros((QROWS, BLOCK), F32)
-    for block in range(PAIR // BLOCK):
+    blocks = PAIR // BLOCK
+    for block in range(blocks):
         here = slice(block * BLOCK, (block + 1) * BLOCK)
         total = gots[0][:, here].astype(F32)
         for got in gots[1:]:
@@ -350,29 +360,47 @@
         top = jnp.max(jnp.abs(update), axis=1, keepdims=True) + scale_epsilon
         scale = jnp.broadcast_to(top.astype(BF16).astype(F32), (QROWS, BLOCK))
         code_ref[:, here] = (update / scale).astype(BF16)
-        scales = jnp.where(lane == block, scale, scales)
-    code_ref[:, PAIR:] = scales.astype(BF16)
+        scales = jnp.where(lane == half * blocks + block, scale, scales)
     if half:
-        for group in range(NEAR):
-            rows = slice(group * OWN, (group + 1) * OWN)
-            momentum_ref[:, column(group)] = before_ref[rows, :]
-            momentum_ref[:, column(NEAR + group)] = sent[rows, :]
-
-
-def outer_step(half, where, outer_momentum, gots, *before):
-    momentum = ((QROWS, PAIR), (OWN, WIDTH))[half]
+        code_ref[:, PAIR:] = scales.astype(BF16)
+    else:
+        scales_ref[...] = scales
+
+
+def outer_step(half, where, outer_momentum, gots, *scales):
+    out_shape = [
+        jax.ShapeDtypeStruct((QROWS, PAIR), F32),
+        jax.ShapeDtypeStruct((QROWS, PAIR + half * BLOCK), BF16),
+    ]
+    if not half:
+        out_shape.append(jax.ShapeDtypeStruct((QROWS, BLOCK), F32))
     return pl.pallas_call(
         functools.partial(outer_kernel, half),
-        out_shape=(
-            jax.ShapeDtypeStruct(momentum, F32),
-            jax.ShapeDtypeStruct((QROWS, PAIR + BLOCK), BF16),
-        ),
-        in_specs=[SM] + [VM] * (5 + len(before)),
-        out_specs=(VM, VM),
-        scratch_shapes=[pltpu.VMEM((QROWS, PAIR), F32)] * (1 + half),
+        out_shape=tuple(out_shape),
+        in_specs=[SM] + [VM] * (5 + len(scales)),
+        out_specs=(VM,) * len(out_shape),
+        scratch_shapes=[pltpu.VMEM((QROWS, PAIR), F32)],
         compiler_params=params(8),
         name="outer_step",
-    )(where, outer_momentum, *gots, *before)
+    )(where, outer_momentum, *gots, *scales)
+
+
+def momentum_kernel(where_ref, near_ref, rest_ref, out_ref):
+    for group in range(NEAR):
+        rows = slice(group * OWN, (group + 1) * OWN)
+        out_ref[:, column(where_ref, group)] = near_ref[rows, :]
+        out_ref[:, column(where_ref, NEAR + group)] = rest_ref[rows, :]
+
+
+def momentum_rows(where, near, rest):
+    return pl.pallas_call(
+        momentum_kernel,
+        out_shape=jax.ShapeDtypeStruct((OWN, WIDTH), F32),
+        in_specs=[SM, VM, VM],
+        out_specs=VM,
+        compiler_params=params(8),
+        name="momentum_rows",
+    )(where, near, rest)
 
 
 def line_kernel(where_ref, *refs):
@@ -392,10 +420,10 @@
 def line_rows(where, *pieces):
     return pl.pallas_call(
         line_kernel,
-        out_shape=jax.ShapeDtypeStruct((NEAR, QROWS, PAIR + BLOCK), BF16),
+        out_shape=jax.ShapeDtypeStruct((NEAR,) + pieces[0].shape, BF16),
         in_specs=[SM] + [VM] * 4,
         out_specs=VM,
-        scratch_shapes=[pltpu.VMEM((ROWS, PAIR + BLOCK), F32)],
+        scratch_shapes=[pltpu.VMEM((ROWS, pieces[0].shape[1]), F32)],
         compiler_params=params(8),
         name="line_rows",
     )(where, *pieces)
@@ -410,14 +438,16 @@
         rows = pl.ds(pl.multiple_of(((x - by + 4) % 4) * QROWS, 8), QROWS)
 
         def slots(group, carry, rows=rows, by=by):
+            scales = pieces[4 + by][group, :, PAIR:].astype(F32)
             for half in range(2):
                 piece = pieces[half * 4 + by]
-                scales = piece[group, :, PAIR:].astype(F32)
+                first = half * (PAIR // BLOCK)
                 base = where_ref[half * NEAR + group] * PAIR
                 for block in range(PAIR // BLOCK):
                     at = pl.ds(pl.multiple_of(base + block * BLOCK, BLOCK), BLOCK)
                     codes = piece[group, :, block * BLOCK : (block + 1) * BLOCK].astype(F32)
-                    new_buf[rows, at] = w_ref[rows, at] - outer_rate * (codes * scales[:, block : block + 1])
+                    value = codes * scales[:, first + block : first + block + 1]
+                    new_buf[rows, at] = w_ref[rows, at] - outer_rate * value
             return carry
 
         lax.fori_loop(0, NEAR, slots, 0)
@@ -470,8 +500,8 @@
     ids = token_ids[0]
     wanted = jnp.transpose(targets[0], (0, 2, 1))
     moments = (first_moment[0], second_moment[0])
-    own1 = gather(0, True, ids, table_t)
-    own2 = gather(1, False, ids, table_t, where)
+    own1 = gather(0, 2, ids, table_t)
+    own2 = gather(1, 1, ids, table_t, where)
 
     far1 = shift(own1, "zh", 1)
     left1, right1 = shift(own1, "y", 1), shift(own1, "y", -1)
@@ -482,11 +512,12 @@
     near1 = swap(pack(own1, far1, left1, right1))
     far_opposite1 = shift(far_right1, "y", -1)
     far_left2 = shift(far2, "y", 1)
-    rest1 = swap(pack(opposite1, far_left1, far_right1, far_opposite1))
+    rest1 = swap(pack(opposite1, far_left1, far_right1))
+    last1 = swap(far_opposite1)
     total, near1 = forward(0, 0, where, (), weight, [near1])
     far_right2 = shift(after(far2, far_opposite1), "y", -1)
     near2 = swap(pack(own2, far2, left2, right2))
-    signal, rest1 = forward(1, 0, where, (total, wanted), weight, [rest1])
+    signal, rest1 = forward(1, 0, where, (total, wanted), weight, [rest1, last1])
     far_opposite2 = shift(far_left2, "y", 1)
     current0, *state0 = first_back(0, where, signal, near1, weight, *moments)
     rest2 = swap(pack(opposite2, far_left2, far_right2))
@@ -499,17 +530,19 @@
     for state, x_half in ((state0, near2), (state1, rest2)):
         sends = second_back(where, signal, x_half, state)
         payloads.append([sends[0]] + shifts(sends[1:], "x"))
-    momentum, pieces = (), []
+    momenta, scales, pieces = [], [], []
     for half in range(2):
         sends = partial_sums(where, payloads[half])
         sums = [sends[0]] + shifts(sends[1:], "zl")
-        *momentum, codes = outer_step(half, where, outer_momentum, sums, *momentum)
+        result = outer_step(half, where, outer_momentum, sums, *scales)
+        momenta.append(result[0])
+        codes, *scales = result[1:]
         line = line_rows(where, codes, *shifts([codes] * 3, "zl"))
         left, right = shift(line, "x", 1), shift(line, "x", 3)
         opposite = shift((left, right)[half], "x", (1, 3)[half])
         pieces += [line, left, opposite, right]
     new_weight = final_step(where, weight, pieces)
-    return (new_weight, momentum[0])
+    return (new_weight, momentum_rows(where, *momenta))
 
 
 def solution(mesh):

time: 183 us -> 175 us (0.956)
  the two profiles are of different devices: /device:TPU:32 before, /device:TPU:24 now
where the time goes in v2:
time: 175 us; the launch traced here: 174 us
  starting transfers between devices  72.1 us (41%)
  waiting for transfers between devices  57.7 us (33%)
  Pallas kernels  40.4 us (23%)
  local copies, waits for them, and re-layouts  2.06 us (1%)
    ppermute x44, starting transfers between devices, shift(): lax.ppermute(value, axis, [(i, (i + by) % size) for i in range(size)])  72.1 us
    ppermute x44, waiting for transfers between devices, shift(): lax.ppermute(value, axis, [(i, (i + by) % size) for i in range(size)])  57.7 us
    pallas_call x2, Pallas kernels, second_back(): pl.pallas_call(second_back_kernel, out_shape=(jax.ShapeDtypeStruct((QROWS...  10.2 us
    pallas_call x2, Pallas kernels, first_back(): pl.pallas_call(functools.partial(first_back_kernel, half), out_shape=(jax...  9.17 us
    pallas_call x4, Pallas kernels, forward(): pl.pallas_call(functools.partial(kernel, counts, step), out_shape=(jax.Sh...  7.96 us
  transfers between devices with their start and end apart: 44, of which 19 were waited for; matrix products, arithmetic and copies ran while one was open for 0% of the time, Pallas kernels for 16%

profile of v2, /device:TPU:24, one launch (start us, length us, event | category | flops | bytes accessed | tf_op | source)
XLA Modules:
  0.0 173.5 jit_solution(12581600480672721301)
XLA Ops:
  3.8 7.3 %collective-permute-start = (bf16[320,512]{1,0:T(8,128)(2,1)S(1)}, bf16[320,512]{1,0:T(8,128)(2,1)S(1)}, u32[]{:S(2)}, u32[]{:S(2)}) collective-permute-start(bf16[320,512]{1,0:T(8,128)(2,1)S(1)} %gather.2.refs_0_), channel_id=1, source_target_pairs={{0,32},{32,0},{1,33},{33,1},{2,34},{34,2},{3,35},{35,3},{4,36},{36... | collective-permute-start | bytes 983048 | tf_op jit(solution)/shard_map/ppermute | solution.py:474
  13.1 6.8 %collective-permute-done.refs_1_ = bf16[320,512]{1,0:T(8,128)(2,1)S(1)} collective-permute-done((bf16[320,512]{1,0:T(8,128)(2,1)S(1)}, bf16[320,512]{1,0:T(8,128)(2,1)S(1)}, u32[]{:S(2)}, u32[]{:S(2)}) %collective-permute-start) | collective-permute-done | bytes 327712 | tf_op jit(solution)/shard_map/ppermute | solution.py:474
  22.7 11.0 %collective-permute-start.10 = (bf16[320,512]{1,0:T(8,128)(2,1)S(1)}, bf16[320,512]{1,0:T(8,128)(2,1)S(1)}, u32[]{:S(2)}, u32[]{:S(2)}) collective-permute-start(bf16[320,512]{1,0:T(8,128)(2,1)S(1)} %gather.3.refs_0_), channel_id=1, source_target_pairs={{0,32},{32,0},{1,33},{33,1},{2,34},{34,2},{3,35},{35,3},{4,36},{36... | collective-permute-start | bytes 983048 | tf_op jit(solution)/shard_map/ppermute | solution.py:474
  34.1 2.8 %collective-permute-start.11 = (bf16[320,512]{1,0:T(8,128)(2,1)S(1)}, bf16[320,512]{1,0:T(8,128)(2,1)S(1)}, u32[]{:S(2)}, u32[]{:S(2)}) collective-permute-start(bf16[320,512]{1,0:T(8,128)(2,1)S(1)} %gather.3.refs_0_), channel_id=1, source_target_pairs={{0,64},{64,128},{128,192},{192,0},{1,65},{65,129},{129,193},{193,1... | collective-permute-start | bytes 983048 | tf_op jit(solution)/shard_map/ppermute | solution.py:474
  36.9 3.2 %collective-permute-start.5 = (bf16[320,512]{1,0:T(8,128)(2,1)S(1)}, bf16[320,512]{1,0:T(8,128)(2,1)S(1)}, u32[]{:S(2)}, u32[]{:S(2)}) collective-permute-start(bf16[320,512]{1,0:T(8,128)(2,1)S(1)} %collective-permute-done.refs_1_), channel_id=1, source_target_pairs={{0,64},{64,128},{128,192},{192,0},{1,65},{65,129},{129,193},{193,1... | collective-permute-start | bytes 983048 | tf_op jit(solution)/shard_map/ppermute | solution.py:474
  40.2 3.4 %collective-permute-done.10.refs_1_ = bf16[320,512]{1,0:T(8,128)(2,1)S(1)} collective-permute-done((bf16[320,512]{1,0:T(8,128)(2,1)S(1)}, bf16[320,512]{1,0:T(8,128)(2,1)S(1)}, u32[]{:S(2)}, u32[]{:S(2)}) %collective-permute-start.10) | collective-permute-done | bytes 327712 | tf_op jit(solution)/shard_map/ppermute | solution.py:474
  48.8 5.6 %collective-permute-done.4.refs_0_ = bf16[320,512]{1,0:T(8,128)(2,1)S(1)} collective-permute-done((bf16[320,512]{1,0:T(8,128)(2,1)S(1)}, bf16[320,512]{1,0:T(8,128)(2,1)S(1)}, u32[]{:S(2)}, u32[]{:S(2)}) %collective-permute-start.4) | collective-permute-done | bytes 327712 | tf_op jit(solution)/shard_map/ppermute | solution.py:474
  59.9 6.2 %collective-permute-done.16.refs_2_ = bf16[320,512]{1,0:T(8,128)(2,1)S(1)} collective-permute-done((bf16[320,512]{1,0:T(8,128)(2,1)S(1)}, bf16[320,512]{1,0:T(8,128)(2,1)S(1)}, u32[]{:S(2)}, u32[]{:S(2)}) %collective-permute-start.16) | collective-permute-done | bytes 327712 | tf_op jit(solution)/shard_map/ppermute | solution.py:474
  66.4 10.0 %collective-permute-done.18.refs_2_ = bf16[320,512]{1,0:T(8,128)(2,1)S(1)} collective-permute-done((bf16[320,512]{1,0:T(8,128)(2,1)S(1)}, bf16[320,512]{1,0:T(8,128)(2,1)S(1)}, u32[]{:S(2)}, u32[]{:S(2)}) %collective-permute-start.18) | collective-permute-done | bytes 327712 | tf_op jit(solution)/shard_map/ppermute | solution.py:474
  81.0 4.6 %first_back.3 = (bf16[160,2560]{1,0:T(8,128)(2,1)S(1)}, f32[160,2560]{1,0:T(8,128)S(1)}, f32[160,2560]{1,0:T(8,128)S(1)}, f32[160,2560]{1,0:T(8,128)S(1)}) custom-call(s32[11]{0:T(128)S(1)} %compare_select_fusion.6.where_ref.refs_0_, bf16[160,512]{1,0:T(8,128)(2,1)S(1)} %get-tuple-element.41.signal_ref, bf16[2560,512]{1,0:T(8,128)(2,1)S(1)} %get-tuple-element.45.x_ref, ...), custom_call_target="tpu_custom_call" | custom-call | flops 419430400 | bytes 14680064 | tf_op jit(solution)/shard_map/first_back/pallas_call | solution.py:241
  85.6 4.6 %first_back.2 = (bf16[160,2560]{1,0:T(8,128)(2,1)S(1)}, f32[160,2560]{1,0:T(8,128)S(1)}, f32[160,2560]{1,0:T(8,128)S(1)}, f32[160,2560]{1,0:T(8,128)S(1)}) custom-call(s32[11]{0:T(128)S(1)} %compare_select_fusion.6.where_ref.refs_0_, bf16[160,512]{1,0:T(8,128)(2,1)S(1)} %get-tuple-element.41.signal_ref, bf16[2560,512]{1,0:T(8,128)(2,1)S(1)} %get-tuple-element.42.x_ref, ...), custom_call_target="tpu_custom_call" | custom-call | flops 419430400 | bytes 14680064 | tf_op jit(solution)/shard_map/first_back/pallas_call | solution.py:241
  94.2 5.1 %second_back.2 = (bf16[40,2688]{1,0:T(8,128)(2,1)S(1)}, bf16[40,2688]{1,0:T(8,128)(2,1)S(1)}, bf16[40,2688]{1,0:T(8,128)(2,1)S(1)}, bf16[40,2688]{1,0:T(8,128)(2,1)S(1)}) custom-call(s32[11]{0:T(128)S(1)} %compare_select_fusion.6.where_ref.refs_0_, bf16[160,512]{1,0:T(8,128)(2,1)S(1)} %get-tuple-element.48.signal_ref, ...), custom_call_target="tpu_custom_call" | custom-call | flops 419430400 | bytes 14680064 | tf_op jit(solution)/shard_map/second_back/pallas_call | solution.py:283
  100.9 2.7 %collective-permute-start.21 = (bf16[40,2688]{1,0:T(8,128)(2,1)S(1)}, bf16[40,2688]{1,0:T(8,128)(2,1)S(1)}, u32[]{:S(2)}, u32[]{:S(2)}) collective-permute-start(bf16[40,2688]{1,0:T(8,128)(2,1)S(1)} %get-tuple-element.55), channel_id=1, source_target_pairs={{0,8},{4,12},{8,0},{12,4},{1,9},{5,13},{9,1},{13,5},{2,10},{6,14},... | collective-permute-start | bytes 645128 | tf_op jit(solution)/shard_map/ppermute | solution.py:474
  105.0 5.1 %second_back.3 = (bf16[40,2688]{1,0:T(8,128)(2,1)S(1)}, bf16[40,2688]{1,0:T(8,128)(2,1)S(1)}, bf16[40,2688]{1,0:T(8,128)(2,1)S(1)}, bf16[40,2688]{1,0:T(8,128)(2,1)S(1)}) custom-call(s32[11]{0:T(128)S(1)} %compare_select_fusion.6.where_ref.refs_0_, bf16[160,512]{1,0:T(8,128)(2,1)S(1)} %get-tuple-element.48.signal_ref, ...), custom_call_target="tpu_custom_call" | custom-call | flops 419430400 | bytes 14680064 | tf_op jit(solution)/shard_map/second_back/pallas_call | solution.py:283
  115.3 3.8 %collective-permute-start.23 = (bf16[40,640]{1,0:T(8,128)(2,1)S(1)}, bf16[40,640]{1,0:T(8,128)(2,1)S(1)}, u32[]{:S(2)}, u32[]{:S(2)}) collective-permute-start(bf16[40,640]{1,0:T(8,128)(2,1)S(1)} %get-tuple-element.58), channel_id=1, source_target_pairs={{0,1},{1,2},{2,3},{3,0},{4,5},{5,6},{6,7},{7,4},{8,9},{9,10},{10,1... | collective-permute-start | bytes 153608 | tf_op jit(solution)/shard_map/ppermute | solution.py:474
  119.8 3.2 %collective-permute-done.32.refs_1_ = bf16[40,2688]{1,0:T(8,128)(2,1)S(1)} collective-permute-done((bf16[40,2688]{1,0:T(8,128)(2,1)S(1)}, bf16[40,2688]{1,0:T(8,128)(2,1)S(1)}, u32[]{:S(2)}, u32[]{:S(2)}) %collective-permute-start.32) | collective-permute-done | bytes 215072 | tf_op jit(solution)/shard_map/ppermute | solution.py:474
  123.0 3.7 %collective-permute-start.25 = (bf16[40,640]{1,0:T(8,128)(2,1)S(1)}, bf16[40,640]{1,0:T(8,128)(2,1)S(1)}, u32[]{:S(2)}, u32[]{:S(2)}) collective-permute-start(bf16[40,640]{1,0:T(8,128)(2,1)S(1)} %get-tuple-element.60), channel_id=1, source_target_pairs={{0,3},{1,0},{2,1},{3,2},{4,7},{5,4},{6,5},{7,6},{8,11},{9,8},{10,9... | collective-permute-start | bytes 153608 | tf_op jit(solution)/shard_map/ppermute | solution.py:474
  128.1 2.6 %collective-permute-start.36 = (bf16[40,640]{1,0:T(8,128)(2,1)S(1)}, bf16[40,640]{1,0:T(8,128)(2,1)S(1)}, u32[]{:S(2)}, u32[]{:S(2)}) collective-permute-start(bf16[40,640]{1,0:T(8,128)(2,1)S(1)} %get-tuple-element.72), channel_id=1, source_target_pairs={{0,2},{1,3},{2,0},{3,1},{4,6},{5,7},{6,4},{7,5},{8,10},{9,11},{10,... | collective-permute-start | bytes 153608 | tf_op jit(solution)/shard_map/ppermute | solution.py:474
  137.3 2.9 %collective-permute-start.39 = (bf16[40,768]{1,0:T(8,128)(2,1)S(1)}, bf16[40,768]{1,0:T(8,128)(2,1)S(1)}, u32[]{:S(2)}, u32[]{:S(2)}) collective-permute-start(bf16[40,768]{1,0:T(8,128)(2,1)S(1)} %get-tuple-element.75.refs_0_), channel_id=1, source_target_pairs={{0,2},{1,3},{2,0},{3,1},{4,6},{5,7},{6,4},{7,5},{8,10},{9,11},{10,... | collective-permute-start | bytes 184328 | tf_op jit(solution)/shard_map/ppermute | solution.py:474
  146.7 2.8 %collective-permute-start.27 = (bf16[40,640]{1,0:T(8,128)(2,1)S(1)}, bf16[40,640]{1,0:T(8,128)(2,1)S(1)}, u32[]{:S(2)}, u32[]{:S(2)}) collective-permute-start(bf16[40,640]{1,0:T(8,128)(2,1)S(1)} %get-tuple-element.61.refs_0_), channel_id=1, source_target_pairs={{0,2},{1,3},{2,0},{3,1},{4,6},{5,7},{6,4},{7,5},{8,10},{9,11},{10,... | collective-permute-start | bytes 153608 | tf_op jit(solution)/shard_map/ppermute | solution.py:474
  155.5 3.1 %collective-permute-start.43 = (bf16[4,40,768]{2,1,0:T(8,128)(2,1)S(1)}, bf16[4,40,768]{2,1,0:T(8,128)(2,1)S(1)}, u32[]{:S(2)}, u32[]{:S(2)}) collective-permute-start(bf16[4,40,768]{2,1,0:T(8,128)(2,1)S(1)} %collective-permute-done.42.refs_7_), channel_id=1, source_target_pairs={{0,12},{4,0},{8,4},{12,8},{1,13},{5,1},{9,5},{13,9},{2,14},{6,2},{... | collective-permute-start | bytes 737288 | tf_op jit(solution)/shard_map/ppermute | solution.py:474
  159.8 3.1 %collective-permute-done.29.refs_1_ = bf16[4,40,640]{2,1,0:T(8,128)(2,1)S(1)} collective-permute-done((bf16[4,40,640]{2,1,0:T(8,128)(2,1)S(1)}, bf16[4,40,640]{2,1,0:T(8,128)(2,1)S(1)}, u32[]{:S(2)}, u32[]{:S(2)}) %collective-permute-start.29) | collective-permute-done | bytes 204832 | tf_op jit(solution)/shard_map/ppermute | solution.py:474
  166.4 3.6 %collective-permute-done.30.refs_2_ = bf16[4,40,640]{2,1,0:T(8,128)(2,1)S(1)} collective-permute-done((bf16[4,40,640]{2,1,0:T(8,128)(2,1)S(1)}, bf16[4,40,640]{2,1,0:T(8,128)(2,1)S(1)}, u32[]{:S(2)}, u32[]{:S(2)}) %collective-permute-start.30) | collective-permute-done | bytes 204832 | tf_op jit(solution)/shard_map/ppermute | solution.py:474
  170.0 3.4 %final_step.1 = f32[160,5120]{1,0:T(8,128)} custom-call(s32[11]{0:T(128)S(1)} %compare_select_fusion.6.where_ref.refs_0_, f32[160,5120]{1,0:T(8,128)S(1)} %copy-done, bf16[4,40,640]{2,1,0:T(8,128)(2,1)S(1)} %line_rows.2.refs_0_, bf16[4,40,640]{2,1,0:T(8,128)(2,1)S(1)} %collective-permute-done.29.refs_1_, ...), custom_call_target="tpu_custom_call" | custom-call | tf_op jit(solution)/shard_map/final_step/pallas_call | solution.py:461
  (109 shorter events, 61.7 us)
Async XLA Ops:
  3.8 16.1 %collective-permute-start = (bf16[320,512]{1,0:T(8,128)(2,1)S(1)}, bf16[320,512]{1,0:T(8,128)(2,1)S(1)}, u32[]{:S(2)}, u32[]{:S(2)}) collective-permute-start(bf16[320,512]{1,0:T(8,128)(2,1)S(1)} %gather.2.refs_0_), channel_id=1, source_target_pairs={{0,32},{32,0},{1,33},{33,1},{2,34},{34,2},{3,35},{35,3},{4,36},{36... | collective-permute-start | bytes 983048 | tf_op jit(solution)/shard_map/ppermute | solution.py:474
  11.1 23.0 %collective-permute-start.1 = (bf16[320,512]{1,0:T(8,128)(2,1)S(1)}, bf16[320,512]{1,0:T(8,128)(2,1)S(1)}, u32[]{:S(2)}, u32[]{:S(2)}) collective-permute-start(bf16[320,512]{1,0:T(8,128)(2,1)S(1)} %gather.2.refs_0_), channel_id=1, source_target_pairs={{0,64},{64,128},{128,192},{192,0},{1,65},{65,129},{129,193},{193,1... | collective-permute-start | bytes 983048 | tf_op jit(solution)/shard_map/ppermute | solution.py:474
  11.3 25.6 %collective-permute-start.2 = (bf16[320,512]{1,0:T(8,128)(2,1)S(1)}, bf16[320,512]{1,0:T(8,128)(2,1)S(1)}, u32[]{:S(2)}, u32[]{:S(2)}) collective-permute-start(bf16[320,512]{1,0:T(8,128)(2,1)S(1)} %gather.2.refs_0_), channel_id=1, source_target_pairs={{0,192},{64,0},{128,64},{192,128},{1,193},{65,1},{129,65},{193,129... | collective-permute-start | bytes 983048 | tf_op jit(solution)/shard_map/ppermute | solution.py:474
  19.9 17.0 %collective-permute-start.6 = (bf16[320,512]{1,0:T(8,128)(2,1)S(1)}, bf16[320,512]{1,0:T(8,128)(2,1)S(1)}, u32[]{:S(2)}, u32[]{:S(2)}) collective-permute-start(bf16[320,512]{1,0:T(8,128)(2,1)S(1)} %collective-permute-done.refs_1_), channel_id=1, source_target_pairs={{0,192},{64,0},{128,64},{192,128},{1,193},{65,1},{129,65},{193,129... | collective-permute-start | bytes 983048 | tf_op jit(solution)/shard_map/ppermute | solution.py:474
  22.7 20.9 %collective-permute-start.10 = (bf16[320,512]{1,0:T(8,128)(2,1)S(1)}, bf16[320,512]{1,0:T(8,128)(2,1)S(1)}, u32[]{:S(2)}, u32[]{:S(2)}) collective-permute-start(bf16[320,512]{1,0:T(8,128)(2,1)S(1)} %gather.3.refs_0_), channel_id=1, source_target_pairs={{0,32},{32,0},{1,33},{33,1},{2,34},{34,2},{3,35},{35,3},{4,36},{36... | collective-permute-start | bytes 983048 | tf_op jit(solution)/shard_map/ppermute | solution.py:474
  33.6 12.5 %collective-permute-start.12 = (bf16[320,512]{1,0:T(8,128)(2,1)S(1)}, bf16[320,512]{1,0:T(8,128)(2,1)S(1)}, u32[]{:S(2)}, u32[]{:S(2)}) collective-permute-start(bf16[320,512]{1,0:T(8,128)(2,1)S(1)} %gather.3.refs_0_), channel_id=1, source_target_pairs={{0,192},{64,0},{128,64},{192,128},{1,193},{65,1},{129,65},{193,129... | collective-permute-start | bytes 983048 | tf_op jit(solution)/shard_map/ppermute | solution.py:474
  34.1 12.0 %collective-permute-start.11 = (bf16[320,512]{1,0:T(8,128)(2,1)S(1)}, bf16[320,512]{1,0:T(8,128)(2,1)S(1)}, u32[]{:S(2)}, u32[]{:S(2)}) collective-permute-start(bf16[320,512]{1,0:T(8,128)(2,1)S(1)} %gather.3.refs_0_), channel_id=1, source_target_pairs={{0,64},{64,128},{128,192},{192,0},{1,65},{65,129},{129,193},{193,1... | collective-permute-start | bytes 983048 | tf_op jit(solution)/shard_map/ppermute | solution.py:474
  46.1 30.3 %collective-permute-start.3 = (bf16[1280,512]{1,0:T(8,128)(2,1)S(1)}, bf16[1280,512]{1,0:T(8,128)(2,1)S(1)}, u32[]{:S(2)}, u32[]{:S(2)}) collective-permute-start(bf16[1280,512]{1,0:T(8,128)(2,1)S(1)} %pack.4.refs_0_), channel_id=1, source_target_pairs={{0,16},{16,0},{1,17},{17,1},{2,18},{18,2},{3,19},{19,3},{4,20},{20... | collective-permute-start | bytes 3932168 | tf_op jit(solution)/shard_map/ppermute | solution.py:474
  46.1 11.8 %collective-permute-start.15 = (bf16[320,512]{1,0:T(8,128)(2,1)S(1)}, bf16[320,512]{1,0:T(8,128)(2,1)S(1)}, u32[]{:S(2)}, u32[]{:S(2)}) collective-permute-start(bf16[320,512]{1,0:T(8,128)(2,1)S(1)} %collective-permute-done.10.refs_1_), channel_id=1, source_target_pairs={{0,64},{64,128},{128,192},{192,0},{1,65},{65,129},{129,193},{193,1... | collective-permute-start | bytes 983048 | tf_op jit(solution)/shard_map/ppermute | solution.py:474
  47.6 42.5 %collective-permute-start.13 = (bf16[1280,512]{1,0:T(8,128)(2,1)S(1)}, bf16[1280,512]{1,0:T(8,128)(2,1)S(1)}, u32[]{:S(2)}, u32[]{:S(2)}) collective-permute-start(bf16[1280,512]{1,0:T(8,128)(2,1)S(1)} %pack.6.refs_0_), channel_id=1, source_target_pairs={{0,16},{16,0},{1,17},{17,1},{2,18},{18,2},{3,19},{19,3},{4,20},{20... | collective-permute-start | bytes 3932168 | tf_op jit(solution)/shard_map/ppermute | solution.py:474
  47.8 12.2 %collective-permute-start.14 = (bf16[320,512]{1,0:T(8,128)(2,1)S(1)}, bf16[320,512]{1,0:T(8,128)(2,1)S(1)}, u32[]{:S(2)}, u32[]{:S(2)}) collective-permute-start(bf16[320,512]{1,0:T(8,128)(2,1)S(1)} %collective-permute-done.12.refs_3_), channel_id=1, source_target_pairs={{0,192},{64,0},{128,64},{192,128},{1,193},{65,1},{129,65},{193,129... | collective-permute-start | bytes 983048 | tf_op jit(solution)/shard_map/ppermute | solution.py:474
  54.4 11.7 %collective-permute-start.16 = (bf16[320,512]{1,0:T(8,128)(2,1)S(1)}, bf16[320,512]{1,0:T(8,128)(2,1)S(1)}, u32[]{:S(2)}, u32[]{:S(2)}) collective-permute-start(bf16[320,512]{1,0:T(8,128)(2,1)S(1)} %collective-permute-done.10.refs_1_), channel_id=1, source_target_pairs={{0,192},{64,0},{128,64},{192,128},{1,193},{65,1},{129,65},{193,129... | collective-permute-start | bytes 983048 | tf_op jit(solution)/shard_map/ppermute | solution.py:474
  57.9 21.0 %collective-permute-start.7 = (bf16[960,512]{1,0:T(8,128)(2,1)S(1)}, bf16[960,512]{1,0:T(8,128)(2,1)S(1)}, u32[]{:S(2)}, u32[]{:S(2)}) collective-permute-start(bf16[960,512]{1,0:T(8,128)(2,1)S(1)} %pack.5.refs_0_), channel_id=1, source_target_pairs={{0,16},{16,0},{1,17},{17,1},{2,18},{18,2},{3,19},{19,3},{4,20},{20... | collective-permute-start | bytes 2949128 | tf_op jit(solution)/shard_map/ppermute | solution.py:474
  66.2 26.0 %collective-permute-start.17 = (bf16[960,512]{1,0:T(8,128)(2,1)S(1)}, bf16[960,512]{1,0:T(8,128)(2,1)S(1)}, u32[]{:S(2)}, u32[]{:S(2)}) collective-permute-start(bf16[960,512]{1,0:T(8,128)(2,1)S(1)} %pack.7.refs_0_), channel_id=1, source_target_pairs={{0,16},{16,0},{1,17},{17,1},{2,18},{18,2},{3,19},{19,3},{4,20},{20... | collective-permute-start | bytes 2949128 | tf_op jit(solution)/shard_map/ppermute | solution.py:474
  76.4 15.8 %collective-permute-start.19 = (bf16[320,512]{1,0:T(8,128)(2,1)S(1)}, bf16[320,512]{1,0:T(8,128)(2,1)S(1)}, u32[]{:S(2)}, u32[]{:S(2)}) collective-permute-start(bf16[320,512]{1,0:T(8,128)(2,1)S(1)} %collective-permute-done.18.refs_2_), channel_id=1, source_target_pairs={{0,16},{16,0},{1,17},{17,1},{2,18},{18,2},{3,19},{19,3},{4,20},{20... | collective-permute-start | bytes 983048 | tf_op jit(solution)/shard_map/ppermute | solution.py:474
  99.3 12.4 %collective-permute-start.20 = (bf16[40,2688]{1,0:T(8,128)(2,1)S(1)}, bf16[40,2688]{1,0:T(8,128)(2,1)S(1)}, u32[]{:S(2)}, u32[]{:S(2)}) collective-permute-start(bf16[40,2688]{1,0:T(8,128)(2,1)S(1)} %get-tuple-element.54), channel_id=1, source_target_pairs={{0,4},{4,8},{8,12},{12,0},{1,5},{5,9},{9,13},{13,1},{2,6},{6,10},{... | collective-permute-start | bytes 645128 | tf_op jit(solution)/shard_map/ppermute | solution.py:474
  100.9 13.5 %collective-permute-start.21 = (bf16[40,2688]{1,0:T(8,128)(2,1)S(1)}, bf16[40,2688]{1,0:T(8,128)(2,1)S(1)}, u32[]{:S(2)}, u32[]{:S(2)}) collective-permute-start(bf16[40,2688]{1,0:T(8,128)(2,1)S(1)} %get-tuple-element.55), channel_id=1, source_target_pairs={{0,8},{4,12},{8,0},{12,4},{1,9},{5,13},{9,1},{13,5},{2,10},{6,14},... | collective-permute-start | bytes 645128 | tf_op jit(solution)/shard_map/ppermute | solution.py:474
  110.2 12.8 %collective-permute-start.32 = (bf16[40,2688]{1,0:T(8,128)(2,1)S(1)}, bf16[40,2688]{1,0:T(8,128)(2,1)S(1)}, u32[]{:S(2)}, u32[]{:S(2)}) collective-permute-start(bf16[40,2688]{1,0:T(8,128)(2,1)S(1)} %get-tuple-element.67), channel_id=1, source_target_pairs={{0,4},{4,8},{8,12},{12,0},{1,5},{5,9},{9,13},{13,1},{2,6},{6,10},{... | collective-permute-start | bytes 645128 | tf_op jit(solution)/shard_map/ppermute | solution.py:474
  110.9 15.9 %collective-permute-start.33 = (bf16[40,2688]{1,0:T(8,128)(2,1)S(1)}, bf16[40,2688]{1,0:T(8,128)(2,1)S(1)}, u32[]{:S(2)}, u32[]{:S(2)}) collective-permute-start(bf16[40,2688]{1,0:T(8,128)(2,1)S(1)} %get-tuple-element.68), channel_id=1, source_target_pairs={{0,8},{4,12},{8,0},{12,4},{1,9},{5,13},{9,1},{13,5},{2,10},{6,14},... | collective-permute-start | bytes 645128 | tf_op jit(solution)/shard_map/ppermute | solution.py:474
  111.7 15.0 %collective-permute-start.34 = (bf16[40,2688]{1,0:T(8,128)(2,1)S(1)}, bf16[40,2688]{1,0:T(8,128)(2,1)S(1)}, u32[]{:S(2)}, u32[]{:S(2)}) collective-permute-start(bf16[40,2688]{1,0:T(8,128)(2,1)S(1)} %get-tuple-element.69), channel_id=1, source_target_pairs={{0,12},{4,0},{8,4},{12,8},{1,13},{5,1},{9,5},{13,9},{2,14},{6,2},{... | collective-permute-start | bytes 645128 | tf_op jit(solution)/shard_map/ppermute | solution.py:474
  115.3 15.3 %collective-permute-start.23 = (bf16[40,640]{1,0:T(8,128)(2,1)S(1)}, bf16[40,640]{1,0:T(8,128)(2,1)S(1)}, u32[]{:S(2)}, u32[]{:S(2)}) collective-permute-start(bf16[40,640]{1,0:T(8,128)(2,1)S(1)} %get-tuple-element.58), channel_id=1, source_target_pairs={{0,1},{1,2},{2,3},{3,0},{4,5},{5,6},{6,7},{7,4},{8,9},{9,10},{10,1... | collective-permute-start | bytes 153608 | tf_op jit(solution)/shard_map/ppermute | solution.py:474
  119.1 13.3 %collective-permute-start.24 = (bf16[40,640]{1,0:T(8,128)(2,1)S(1)}, bf16[40,640]{1,0:T(8,128)(2,1)S(1)}, u32[]{:S(2)}, u32[]{:S(2)}) collective-permute-start(bf16[40,640]{1,0:T(8,128)(2,1)S(1)} %get-tuple-element.59), channel_id=1, source_target_pairs={{0,2},{1,3},{2,0},{3,1},{4,6},{5,7},{6,4},{7,5},{8,10},{9,11},{10,... | collective-permute-start | bytes 153608 | tf_op jit(solution)/shard_map/ppermute | solution.py:474
  155.5 10.9 %collective-permute-start.41 = (bf16[4,40,768]{2,1,0:T(8,128)(2,1)S(1)}, bf16[4,40,768]{2,1,0:T(8,128)(2,1)S(1)}, u32[]{:S(2)}, u32[]{:S(2)}) collective-permute-start(bf16[4,40,768]{2,1,0:T(8,128)(2,1)S(1)} %line_rows.3.refs_4_), channel_id=1, source_target_pairs={{0,4},{4,8},{8,12},{12,0},{1,5},{5,9},{9,13},{13,1},{2,6},{6,10},{... | collective-permute-start | bytes 737288 | tf_op jit(solution)/shard_map/ppermute | solution.py:474
  155.5 14.4 %collective-permute-start.43 = (bf16[4,40,768]{2,1,0:T(8,128)(2,1)S(1)}, bf16[4,40,768]{2,1,0:T(8,128)(2,1)S(1)}, u32[]{:S(2)}, u32[]{:S(2)}) collective-permute-start(bf16[4,40,768]{2,1,0:T(8,128)(2,1)S(1)} %collective-permute-done.42.refs_7_), channel_id=1, source_target_pairs={{0,12},{4,0},{8,4},{12,8},{1,13},{5,1},{9,5},{13,9},{2,14},{6,2},{... | collective-permute-start | bytes 737288 | tf_op jit(solution)/shard_map/ppermute | solution.py:474
  (31 other events, 291.5 us)
